TPU v7x, 32 devices: a whole 2x2x4 slice. The times are simulated.
32 devices in a mesh: groups: 2 (over y), shot: 4 (over z), rcv: 2 (over x), rep: 2 (over core).
Axes of the slice: x: 2, y: 2, z: 4, core: 2. Of those that a mesh axis runs over, the one named last changes fastest.
Arguments:
- records: float32 [64, 131072], P(('groups', 'rcv'), ('shot', 'rep')), parts along dimension 0, may hold values from -6 to 6
- offsets: int32 [16, 32], P(('groups', 'shot', 'rep')), parts along dimension 0, may hold values from 0 to 130560, as said below
- filter_index: int32 [16, 32], P(('groups', 'shot', 'rep')), parts along dimension 0, may hold values from 0 to 7
- signatures: bfloat16 [8, 128], replicated, may hold values from -0.5 to 0.5
- thresholds: float32 [2, 256], replicated, may hold values from 0.3 to 2
Outputs:
- model_field: float32 [16, 32, 32, 512], P(('groups', 'shot', 'rep'), 'rcv'), parts along dimension 0
- residual: float32 [64, 131072], P(('groups', 'rcv'), ('shot', 'rep')), parts along dimension 0
There are 2 independent parts, one for each index of `groups`. A program takes and returns all parts, laid end to end along the dimension named above; an argument that names none is the same for every part. Nothing has to cross between parts.
Inputs may be any that keep to these rules, and one draw needn't show every extreme that they name: Every offset is a multiple of 128. Shot (x,y) starts in slab offsets[x,y] // 16384; within one row x of the shot grid at most 8 shots start in any one slab, and this bound is reached in every row. Every shot ends inside the record.
All inputs are finite; a program needn't handle non-finite values.
Results may differ from a plain program's by a relative error of at most 0.024.
Values may be sent and summed in bfloat16 or wider, within the bound.
A program may use at most 64 MiB of HBM per device.

v0:
```python
import functools
import math

import jax
import jax.numpy as jnp
import numpy as np
from jax import lax
from jax.experimental import pallas as pl
from jax.experimental.pallas import tpu as pltpu
from jax.sharding import PartitionSpec as P

NT = 512


def from_behind(value, axis, steps):
    count = lax.axis_size(axis)
    first, last = (max(0, -steps), min(count, count - steps))
    return lax.ppermute(value, axis, [(source, source + steps) for source in range(first, last)])


def time_table(count):
    samples = jnp.arange(count)
    bin_index = jnp.arange(count // 2)[:, None]
    angles = 2.0 * math.pi / count * (bin_index * samples[None, :] % count).astype(jnp.float32)
    parity = jnp.where(samples % 2 == 0, 1.0, -1.0).astype(jnp.float32)
    cosine = jnp.where(bin_index == 0, math.sqrt(1.0 / count), math.sqrt(2.0 / count)) * jnp.cos(
        angles
    )
    sine_part = jnp.where(
        bin_index == 0,
        math.sqrt(1.0 / count) * parity[None, :],
        -math.sqrt(2.0 / count) * jnp.sin(angles),
    )
    return jnp.stack([cosine, sine_part]).astype(jnp.bfloat16)


def shot_table(count):
    positions = jnp.arange(count)
    angles = (
        2.0
        * math.pi
        / count
        * (positions[:, None] * positions[None, :] % count).astype(jnp.float32)
    )
    scaling = 1.0 / math.sqrt(count)
    cosine = scaling * jnp.cos(angles)
    sine_part = scaling * jnp.sin(angles)
    upper_half = jnp.stack([cosine, sine_part], axis=1)
    lower_half = jnp.stack([-sine_part, cosine], axis=1)
    return jnp.stack([upper_half, lower_half]).astype(jnp.bfloat16)


def toeplitz_kernel(taps_ref, forward_ref, adjoint_ref):
    tap_count = taps_ref.shape[1]
    row_index = lax.broadcasted_iota(jnp.int32, (tap_count, tap_count), 0)
    col_index = lax.broadcasted_iota(jnp.int32, (tap_count, tap_count), 1)
    for index in range(taps_ref.shape[0]):
        row = jnp.broadcast_to(taps_ref[index : index + 1, :], (tap_count, tap_count))
        turned = pltpu.roll(row, 0, 1, stride=1, stride_axis=0)
        zeros = jnp.zeros_like(turned)
        near = jnp.where(col_index >= row_index, turned, zeros)
        far = jnp.where(col_index < row_index, turned, zeros)
        forward_ref[index, :tap_count, :] = near.astype(jnp.bfloat16)
        forward_ref[index, tap_count:, :] = far.astype(jnp.bfloat16)
        adjoint_ref[index, :tap_count, :] = near.T.astype(jnp.bfloat16)
        adjoint_ref[index, tap_count:, :] = far.T.astype(jnp.bfloat16)


def toeplitz_tables(signatures):
    count, tap_count = signatures.shape
    shape = jax.ShapeDtypeStruct((count, 2 * tap_count, tap_count), jnp.bfloat16)
    return pl.pallas_call(
        toeplitz_kernel,
        out_shape=(shape, shape),
        in_specs=[pl.BlockSpec(memory_space=pltpu.VMEM)],
        out_specs=(pl.BlockSpec(memory_space=pltpu.VMEM),) * 2,
    )(signatures.astype(jnp.float32))


def apply_filter(traces, table, adjoint):
    empty = jnp.zeros_like(traces[:, :1])
    if adjoint:
        other = jnp.concatenate([traces[:, 1:], empty], axis=1)
    else:
        other = jnp.concatenate([empty, traces[:, :-1]], axis=1)
    return jnp.einsum(
        "sbrp,spq->sbrq",
        jnp.concatenate([traces, other], axis=3),
        table,
        preferred_element_type=jnp.float32,
    )


def rank_in_row(owners):
    shot_count = owners.shape[1]
    same_owner = owners[:, :, None] == owners[:, None, :]
    earlier = jnp.arange(shot_count)[None, :] < jnp.arange(shot_count)[:, None]
    return jnp.sum(same_owner & earlier[None], axis=2)


def to_slabs(payload):
    return lax.all_to_all(payload, ("shot", "rep"), split_axis=0, concat_axis=0, tiled=True)


def to_shots(payload):
    return lax.all_to_all(payload, ("shot", "rep"), split_axis=0, concat_axis=0, tiled=True)


def soft_limit(coefficients, threshold_row):
    magnitude = jnp.sqrt(coefficients[0] * coefficients[0] + coefficients[1] * coefficients[1])
    threshold_view = threshold_row[None, :, None, None]
    factor = 1.0 - threshold_view / jnp.maximum(magnitude, threshold_view)
    return (coefficients * factor[None]).astype(jnp.bfloat16)


def shrink(field_data, threshold_row, tables):
    table_time, table_x, table_y, table_r = tables
    rows_here, local_rcv, shot_count, sample_count = field_data.shape
    spectrum = jnp.einsum(
        "ckt,xryt->xckry",
        table_time,
        field_data.astype(jnp.bfloat16),
        preferred_element_type=jnp.float32,
    ).astype(jnp.bfloat16)
    bin_count = spectrum.shape[2]
    spectrum = spectrum.reshape(rows_here, 2, bin_count, local_rcv * shot_count)
    section_data = jnp.einsum(
        "akbx,xbfz->akfz",
        table_x,
        lax.all_to_all(spectrum, ("shot", "rep"), split_axis=2, concat_axis=0, tiled=True),
        preferred_element_type=jnp.float32,
    ).astype(jnp.bfloat16)
    all_rows, row_bins = (section_data.shape[1], section_data.shape[2])
    section_data = section_data.reshape(2, all_rows, row_bins, local_rcv, shot_count)
    section_data = lax.all_to_all(section_data, "rcv", split_axis=2, concat_axis=3, tiled=True)
    section_data = jnp.einsum(
        "ajby,bkfry->akfrj", table_y, section_data, preferred_element_type=jnp.float32
    ).astype(jnp.bfloat16)
    coefficients = jnp.einsum(
        "aqbr,bkfrj->akfqj", table_r, section_data, preferred_element_type=jnp.float32
    )
    shrunk = soft_limit(coefficients, threshold_row)
    section_data = jnp.einsum(
        "aqbr,akfqj->bkfrj", table_r, shrunk, preferred_element_type=jnp.float32
    ).astype(jnp.bfloat16)
    section_data = jnp.einsum(
        "ajby,akfrj->bkfry", table_y, section_data, preferred_element_type=jnp.float32
    ).astype(jnp.bfloat16)
    section_data = lax.all_to_all(section_data, "rcv", split_axis=3, concat_axis=2, tiled=True)
    section_data = section_data.reshape(2, all_rows, row_bins, local_rcv * shot_count)
    section_data = jnp.einsum(
        "akbx,akfz->bxfz", table_x, section_data, preferred_element_type=jnp.float32
    ).astype(jnp.bfloat16)
    result = jnp.einsum(
        "ckt,cxkz->xzt",
        table_time,
        lax.all_to_all(section_data, ("shot", "rep"), split_axis=1, concat_axis=2, tiled=True),
        preferred_element_type=jnp.float32,
    )
    return result.reshape(rows_here, local_rcv, shot_count, sample_count)


def body_by_rows(records, offsets, filter_index, signatures, thresholds):
    rows_here, shot_count = offsets.shape
    local_rcv, slab_len = records.shape
    slab_count = lax.axis_size(("shot", "rep"))
    rcv_count = lax.axis_size("rcv")
    tap_count = signatures.shape[1]
    sample_count = NT
    slab_blocks = slab_len // tap_count
    trace_blocks = sample_count // tap_count
    capacity = max(2, 2 * shot_count // slab_count)
    slot_count = slab_count * rows_here * capacity
    forward_tables, adjoint_tables = toeplitz_tables(signatures)
    flat_index = filter_index.reshape(-1)
    forward_table = forward_tables[flat_index]
    adjoint_table = adjoint_tables[flat_index]
    owners = offsets // slab_len
    row_ids = jnp.arange(rows_here, dtype=jnp.int32)[:, None]
    slot_index = (
        owners * (rows_here * capacity) + row_ids * capacity + rank_in_row(owners)
    ).reshape(-1)
    every_offset = lax.all_gather(offsets, ("shot", "rep"), axis=0, tiled=True)
    every_owner = every_offset // slab_len
    every_start = every_offset // tap_count % slab_blocks
    every_rank = rank_in_row(every_owner)
    mine_mask = every_owner == lax.axis_index(("shot", "rep"))
    levels = jnp.arange(capacity, dtype=jnp.int32)
    picked = mine_mask[:, :, None] & (every_rank[:, :, None] == levels[None, None, :])
    table_in = jnp.sum(jnp.where(picked, every_start[:, :, None] + 1, 0), axis=1).reshape(-1)
    filled = table_in > 0
    block_steps = jnp.arange(trace_blocks, dtype=jnp.int32)
    target = jnp.where(
        filled[:, None],
        table_in[:, None] - 1 + block_steps[None, :],
        slab_blocks + trace_blocks - 1,
    )

    def correlate(record_field):
        record_low = (
            record_field.astype(jnp.bfloat16)
            .reshape(local_rcv, slab_blocks, tap_count)
            .transpose(1, 0, 2)
        )
        rim_blocks = from_behind(record_low[: trace_blocks - 1], ("shot", "rep"), -1)
        extended = jnp.concatenate(
            [record_low, rim_blocks, jnp.zeros((1, local_rcv, tap_count), jnp.bfloat16)], axis=0
        )
        windows = extended[target.reshape(-1)].reshape(
            slot_count, trace_blocks, local_rcv, tap_count
        )
        returned = to_shots(windows)
        traces = returned[slot_index]
        terms = apply_filter(traces, adjoint_table, True)
        terms = terms.reshape(rows_here, shot_count, trace_blocks, local_rcv, tap_count).transpose(
            0, 3, 1, 2, 4
        )
        return terms.reshape(rows_here, local_rcv, shot_count, sample_count)

    tables = (
        time_table(sample_count),
        shot_table(slab_count * rows_here),
        shot_table(shot_count),
        shot_table(local_rcv * rcv_count),
    )
    row_bins = sample_count // 2 // slab_count
    rcv_bins = row_bins // rcv_count
    bin_start = lax.axis_index(("shot", "rep")) * row_bins + lax.axis_index("rcv") * rcv_bins

    def threshold_for(level_index):
        return lax.dynamic_slice_in_dim(thresholds[level_index], bin_start, rcv_bins)

    model_field = shrink(correlate(records), threshold_for(0), tables)
    level_index = 1
    traces = model_field.astype(jnp.bfloat16).reshape(
        rows_here, local_rcv, shot_count, trace_blocks, tap_count
    )
    traces = traces.transpose(0, 2, 3, 1, 4).reshape(
        rows_here * shot_count, trace_blocks, local_rcv, tap_count
    )
    shots = apply_filter(traces, forward_table, False).astype(jnp.bfloat16)
    outgoing = (
        jnp.zeros((slot_count, trace_blocks, local_rcv, tap_count), jnp.bfloat16)
        .at[slot_index]
        .set(shots)
    )
    arrived = to_slabs(outgoing)
    slab_total = jnp.zeros((slab_blocks + trace_blocks, local_rcv, tap_count), jnp.float32)
    for block_step in range(trace_blocks):
        slab_total = slab_total.at[target[:, block_step]].add(
            arrived[:, block_step].astype(jnp.float32)
        )
    spill_over = slab_total[slab_blocks : slab_blocks + trace_blocks - 1]
    carried = from_behind(spill_over, ("shot", "rep"), 1)
    blended = slab_total[:slab_blocks].at[: trace_blocks - 1].add(carried)
    residual = records - blended.transpose(1, 0, 2).reshape(local_rcv, slab_len)
    model_field = shrink(model_field + correlate(residual), threshold_for(level_index), tables)
    return (model_field, residual)


def dot(left, right, left_dim=1, right_dim=0):
    return lax.dot_general(
        left, right, (((left_dim,), (right_dim,)), ((), ())), preferred_element_type=jnp.float32
    )


def fixed_time_table(count):
    samples = np.arange(count)
    bins = np.arange(count // 2)[:, None]
    angles = 2.0 * np.pi / count * (bins * samples[None, :] % count)
    scale = math.sqrt(2.0 / count)
    cosine = scale * np.cos(angles)
    sine = -scale * np.sin(angles)
    cosine[0] = math.sqrt(1.0 / count)
    sine[0] = math.sqrt(1.0 / count) * np.where(samples % 2 == 0, 1.0, -1.0)
    return np.stack([cosine, sine]).astype(jnp.bfloat16)


def fixed_shot_table(count):
    positions = np.arange(count)
    angles = 2.0 * np.pi / count * (positions[:, None] * positions[None, :] % count)
    cosine = np.cos(angles) / math.sqrt(count)
    sine = np.sin(angles) / math.sqrt(count)
    table = np.stack([np.stack([cosine, sine], 1), np.stack([-sine, cosine], 1)])
    return table.astype(jnp.bfloat16).astype(np.float32)


def correlate_kernel(starts_ref, picks_ref, blocks_ref, tables_ref, out_ref):
    slots, rows, taps = out_ref.shape
    rcv = blocks_ref.shape[1]
    steps = rows // rcv

    def one(slot, carry):
        window = blocks_ref[pl.ds(starts_ref[slot], steps)].reshape(rows, taps)
        later = jnp.concatenate([window[rcv:], jnp.zeros((rcv, taps), window.dtype)], axis=0)
        pair = jnp.concatenate([window, later], axis=1)
        out_ref[slot] = dot(pair, tables_ref[picks_ref[slot]]).astype(out_ref.dtype)
        return carry

    lax.fori_loop(0, slots, one, 0, unroll=4)


def blend_kernel(starts_ref, picks_ref, traces_ref, tables_ref, out_ref):
    slots, rows, taps = traces_ref.shape
    rcv = out_ref.shape[1]
    steps = rows // rcv
    out_ref[...] = jnp.zeros_like(out_ref)

    def one(slot, carry):
        trace = traces_ref[slot]
        earlier = jnp.concatenate([jnp.zeros((rcv, taps), trace.dtype), trace[:-rcv]], axis=0)
        pair = jnp.concatenate([trace, earlier], axis=1)
        shot = dot(pair, tables_ref[picks_ref[slot]]).astype(jnp.bfloat16).astype(jnp.float32)
        where = pl.ds(starts_ref[slot], steps)
        out_ref[where] = out_ref[where] + shot.reshape(steps, rcv, taps)
        return carry

    lax.fori_loop(0, slots, one, 0, unroll=4)


def slot_call(kernel, out_shape, starts, picks, data, tables):
    vmem = pl.BlockSpec(memory_space=pltpu.VMEM)
    smem = pl.BlockSpec(memory_space=pltpu.SMEM)
    return pl.pallas_call(
        kernel,
        out_shape=out_shape,
        in_specs=[smem, smem, vmem, vmem],
        out_specs=vmem,
    )(starts, picks, data, tables)


def spectrum_kernel(traces_ref, table_ref, out_ref):
    parts, _, bins, _ = out_ref.shape
    both = dot(table_ref[...], traces_ref[0], 1, 1)
    half = parts * bins
    joined = jnp.concatenate([both[:half], both[half:]], axis=1)
    out_ref[:, 0] = joined.reshape(parts, bins, joined.shape[1]).astype(jnp.bfloat16)


def spectrum(traces, table, parts):
    rcv, slots, samples = traces.shape
    bins = samples // 2 // parts
    return pl.pallas_call(
        spectrum_kernel,
        grid=(rcv,),
        out_shape=jax.ShapeDtypeStruct((parts, rcv, bins, 2 * slots), jnp.bfloat16),
        in_specs=[
            pl.BlockSpec((1, slots, samples), lambda i: (i, 0, 0)),
            pl.BlockSpec((samples, samples), lambda i: (0, 0)),
        ],
        out_specs=pl.BlockSpec((parts, 1, bins, 2 * slots), lambda i: (0, i, 0, 0)),
    )(traces, table)


def record_kernel(spectra_ref, table_ref, out_ref):
    parts, _, bins, lanes = spectra_ref.shape
    half = parts * bins
    groups, _, count, _ = out_ref.shape
    values = spectra_ref[:, 0].reshape(half, lanes)
    first = dot(values, table_ref[:half], 0, 0)
    second = dot(values, table_ref[half:], 0, 0)
    for group in range(groups):
        low = 2 * group * count
        out_ref[group, 0] = first[low : low + count] + second[low + count : low + 2 * count]


def records_of(spectra, table, groups):
    parts, rcv, bins, lanes = spectra.shape
    samples = table.shape[1]
    count = lanes // 2 // groups
    return pl.pallas_call(
        record_kernel,
        grid=(rcv,),
        out_shape=jax.ShapeDtypeStruct((groups, rcv, count, samples), jnp.float32),
        in_specs=[
            pl.BlockSpec((parts, 1, bins, lanes), lambda i: (0, i, 0, 0)),
            pl.BlockSpec((samples, samples), lambda i: (0, 0)),
        ],
        out_specs=pl.BlockSpec((groups, 1, count, samples), lambda i: (0, i, 0, 0)),
    )(spectra, table)


def bins_kernel(place, halves, spectra_ref, go_ref, back_ref, cosine_ref, sine_ref, level_ref, out_ref):
    _, rcv, bins, lanes = spectra_ref.shape
    rows = rcv * bins
    rcv_count, slab_count = place.shape
    joined = jnp.concatenate(
        [
            jnp.concatenate(
                [spectra_ref[int(index)].reshape(rows, lanes) for index in line], axis=1
            )
            for line in place
        ],
        axis=0,
    )
    section = dot(joined, go_ref[...]).astype(jnp.bfloat16)
    half = section.shape[1] // 2
    near = dot(cosine_ref[...], section)
    far = dot(sine_ref[...], section)
    real = near[:, :half] + far[:, half:]
    imag = near[:, half:] - far[:, :half]
    level = level_ref[...]
    factor = 1.0 - level / jnp.maximum(jnp.sqrt(real * real + imag * imag), level)
    shrunk = jnp.concatenate([real * factor, imag * factor], axis=1).astype(jnp.bfloat16)
    near = dot(cosine_ref[...], shrunk)
    far = dot(sine_ref[...], shrunk)
    section = jnp.concatenate(
        [near[:, :half] - far[:, half:], far[:, :half] + near[:, half:]], axis=1
    ).astype(jnp.bfloat16)
    result = dot(section, back_ref[...], 1, 1).astype(jnp.bfloat16)
    width = result.shape[1] // slab_count
    for line in range(rcv_count):
        for slab in range(slab_count):
            piece = result[line * rows : (line + 1) * rows, slab * width : (slab + 1) * width]
            if halves == 2:
                piece = jnp.concatenate([piece[: rows // 2], piece[rows // 2 :]], axis=1)
            out_ref[int(place[line, slab])] = piece.reshape(rcv // halves, bins, halves * width)


def bins_stage(spectra, go, back, cosine, sine, level, place, halves):
    parts, rcv, bins, _ = spectra.shape
    width = halves * back.shape[0] // place.shape[1]
    vmem = pl.BlockSpec(memory_space=pltpu.VMEM)
    return pl.pallas_call(
        functools.partial(bins_kernel, place, halves),
        out_shape=jax.ShapeDtypeStruct((parts, rcv // halves, bins, width), jnp.bfloat16),
        in_specs=[vmem] * 6,
        out_specs=vmem,
    )(spectra, go, back, cosine, sine, level)


def body_by_slots(records, offsets, filter_index, signatures, thresholds):
    rows_here, shot_count = offsets.shape
    local_rcv, slab_len = records.shape
    slab_count = lax.axis_size(("shot", "rep"))
    rep_count = lax.axis_size("rep")
    rcv_count = lax.axis_size("rcv")
    parts = slab_count * rcv_count
    everyone = ("shot", "rcv", "rep")
    tap_count = signatures.shape[1]
    slab_blocks = slab_len // tap_count
    steps = NT // tap_count
    capacity = max(2, 2 * shot_count // slab_count)
    row_count = rows_here * slab_count
    slots = row_count * capacity
    bins = NT // 2 // parts
    place = np.array(
        [
            [((slab // rep_count) * rcv_count + line) * rep_count + slab % rep_count for slab in range(slab_count)]
            for line in range(rcv_count)
        ]
    )

    time_table_fixed = jnp.asarray(fixed_time_table(NT).reshape(NT, NT))
    table_x, table_y, table_r = (
        fixed_shot_table(count) for count in (row_count, shot_count, local_rcv * rcv_count)
    )
    grid_table = np.einsum("ajby,bkcx->cxyakj", table_y, table_x).astype(jnp.bfloat16)
    row_table = np.ascontiguousarray(grid_table.transpose(1, 0, 2, 3, 4, 5))
    points = 2 * row_count * shot_count
    grid_table = jnp.asarray(grid_table.reshape(points, points))
    row_table = jnp.asarray(row_table.reshape(points, points))
    same = np.eye(bins, dtype=np.float32)
    cosine = jnp.asarray(np.kron(table_r[0, :, 0], same).astype(jnp.bfloat16))
    sine = jnp.asarray(np.kron(table_r[0, :, 1], same).astype(jnp.bfloat16))

    shots = jnp.stack([offsets, filter_index])
    every = lax.all_to_all(
        jnp.broadcast_to(shots[None], (slab_count,) + shots.shape), ("shot", "rep"), 0, 0, tiled=True
    )
    every_offset = every[:, 0].reshape(row_count, shot_count)
    every_pick = every[:, 1].reshape(row_count, shot_count)
    every_owner = every_offset // slab_len
    every_rank = rank_in_row(every_owner)
    slabs = jnp.arange(slab_count, dtype=jnp.int32)
    ranks = jnp.arange(capacity, dtype=jnp.int32)
    taken = (every_owner[None, :, None, :] == slabs[:, None, None, None]) & (
        every_rank[None, :, None, :] == ranks[None, None, :, None]
    )
    point_of = jnp.arange(row_count * shot_count, dtype=jnp.int32).reshape(row_count, shot_count)
    code = jnp.sum(jnp.where(taken, point_of[None, :, None, :] + 1, 0), axis=3).reshape(
        slab_count, 1, slots
    )
    code = jnp.where(
        code > 0, code - 1 + row_count * shot_count * jnp.arange(2, dtype=jnp.int32)[None, :, None], -1
    ).reshape(-1)
    chosen = (code[:, None] == jnp.arange(points, dtype=jnp.int32)[None, :]).astype(jnp.bfloat16)
    slot_table = dot(chosen, grid_table).astype(jnp.bfloat16)
    mine = (every_owner == lax.axis_index(("shot", "rep")))[:, None, :] & (
        every_rank[:, None, :] == ranks[None, :, None]
    )
    every_start = every_offset // tap_count % slab_blocks
    starts = jnp.sum(jnp.where(mine, every_start[:, None, :], 0), axis=2).reshape(-1)
    picks = jnp.sum(jnp.where(mine, every_pick[:, None, :], 0), axis=2).reshape(-1)
    forward_tables, adjoint_tables = toeplitz_tables(signatures)

    def correlate(blocks, dtype):
        low = blocks.astype(jnp.bfloat16)
        rim = from_behind(low[: steps - 1], ("shot", "rep"), -1)
        extended = jnp.concatenate([low, rim, jnp.zeros_like(low[:1])], axis=0)
        shape = jax.ShapeDtypeStruct((slots, steps * local_rcv, tap_count), dtype)
        terms = slot_call(correlate_kernel, shape, starts, picks, extended, adjoint_tables)
        terms = terms.reshape(slots, steps, local_rcv, tap_count).transpose(2, 0, 1, 3)
        return terms.reshape(local_rcv, slots, NT)

    bin_start = lax.axis_index(everyone) * bins

    def swap(value):
        return lax.all_to_all(value, everyone, 0, 0, tiled=True)

    def shrink_at(traces, index, back, halves):
        level = lax.dynamic_slice_in_dim(thresholds[index], bin_start, bins)
        level = jnp.tile(level, local_rcv * rcv_count)[:, None]
        spectra = swap(spectrum(traces, time_table_fixed, parts))
        spectra = swap(
            bins_stage(spectra, slot_table, back, cosine, sine, level, place, halves)
        )
        return records_of(spectra, time_table_fixed, halves)

    record_blocks = records.reshape(local_rcv, slab_blocks, tap_count).transpose(1, 0, 2)
    model = shrink_at(correlate(record_blocks, jnp.bfloat16), 0, slot_table, 1)[0]
    traces = model.astype(jnp.bfloat16).reshape(local_rcv, slots, steps, tap_count)
    traces = traces.transpose(1, 2, 0, 3).reshape(slots, steps * local_rcv, tap_count)
    shape = jax.ShapeDtypeStruct((slab_blocks + steps, local_rcv, tap_count), jnp.float32)
    total = slot_call(blend_kernel, shape, starts, picks, traces, forward_tables)
    carried = from_behind(total[slab_blocks : slab_blocks + steps - 1], ("shot", "rep"), 1)
    blended = total[:slab_blocks].at[: steps - 1].add(carried)
    left = record_blocks - blended
    residual = left.transpose(1, 0, 2).reshape(local_rcv, slab_len)
    traces = (model + correlate(left, jnp.float32)).astype(jnp.bfloat16)
    model = shrink_at(traces, 1, row_table, 2)
    return (model.reshape(rows_here, local_rcv, shot_count, NT), residual)


def body(records, offsets, filter_index, signatures, thresholds):
    rows_here, shot_count = offsets.shape
    slab_count = lax.axis_size(("shot", "rep"))
    parts = slab_count * lax.axis_size("rcv")
    slots = rows_here * slab_count * max(2, 2 * shot_count // slab_count)
    table_rows = 2 * rows_here * slab_count * shot_count
    fits = table_rows <= 1024 and rows_here == 1 and slots == 64 and 4 * shot_count == 128
    fits = fits and records.shape[0] == 16 and NT // 2 // parts == 16
    run = body_by_slots if fits else body_by_rows
    return run(records, offsets, filter_index, signatures, thresholds)


def solution(mesh):
    in_specs = (
        P(("groups", "rcv"), ("shot", "rep")),
        P(("groups", "shot", "rep"), None),
        P(("groups", "shot", "rep"), None),
        P(),
        P(),
    )
    out_specs = (
        P(("groups", "shot", "rep"), "rcv", None, None),
        P(("groups", "rcv"), ("shot", "rep")),
    )
    return jax.shard_map(body, mesh=mesh, in_specs=in_specs, out_specs=out_specs, check_vma=False)
```

profile of v0, /device:TPU:0, one launch (start us, length us, event | category | flops | bytes accessed | tf_op | source)
XLA Modules:
  0.0 225.9 jit_solution(1951979488357555477)
XLA Ops:
  0.6 0.8 pad_add_fusion
  1.4 0.6 broadcast_in_dim.68
  2.0 6.4 %all-to-all-start = ((s32[8,2,1,32]{3,2,1,0:T(1,128)}), s32[8,2,1,32]{3,2,1,0:T(1,128)S(1)}, u32[]{:S(2)}, u32[]{:S(2)}) async-start(s32[8,2,1,32]{3,2,1,0:T(1,128)} %broadcast_in_dim.68), calls=%async_computation | async-start | bytes 16384 | tf_op jit(solution)/shard_map/all_to_all | solution.py:468
  8.5 1.3 collective-permute-start
  9.8 1.3 convert_element_type.28.taps_ref
  11.1 1.8 shard_map.113
  13.0 1.0 all-to-all-done
  14.7 0.6 reshape.291.starts_ref
  15.3 0.7 reshape.292.picks_ref
  15.9 1.0 maximum_maximum_fusion.blocks_ref
  16.9 5.1 %shard_map.114 = bf16[64,64,128]{2,1,0:T(8,128)(2,1)} custom-call(s32[64]{0:T(128)} %reshape.291.starts_ref, s32[64]{0:T(128)} %reshape.292.picks_ref, bf16[132,16,128]{2,1,0:T(8,128)(2,1)} %maximum_maximum_fusion.blocks_ref, bf16[8,256,128]{2,1,0:T(8,128)(2,1)} %get-tuple-element.16.tables_ref), custom_call_target="tpu_custom_call" | custom-call | tf_op jit(solution)/shard_map/pallas_call | solution.py:324
  22.0 1.7 copy.49
  23.8 1.2 reshape.295.traces_ref
  25.0 11.4 %shard_map.115 = bf16[16,16,16,128]{3,2,1,0:T(8,128)(2,1)} custom-call(bf16[16,64,512]{2,1,0:T(8,128)(2,1)} %reshape.295.traces_ref, bf16[512,512]{1,0:T(8,128)(2,1)} %constant.109.clone.table_ref), custom_call_target="tpu_custom_call" | custom-call | tf_op jit(solution)/shard_map/pallas_call | solution.py:343
  36.4 6.0 %all-to-all-start.1 = ((bf16[16,16,16,128]{3,2,1,0:T(8,128)(2,1)}), bf16[16,16,16,128]{3,2,1,0:T(8,128)(2,1)S(1)}, u32[]{:S(2)}, u32[]{:S(2)}) async-start(bf16[16,16,16,128]{3,2,1,0:T(8,128)(2,1)} %shard_map.115), calls=%async_computation.1 | async-start | bytes 2097152 | tf_op jit(solution)/shard_map/all_to_all | solution.py:509
  42.5 0.9 broadcast_in_dim_tile.8.level_ref
  43.4 1.2 select_reduce_fusion
  44.9 1.7 fusion.2.go_ref.back_ref
  46.6 18.6 %all-to-all-done.1.spectra_ref = bf16[16,16,16,128]{3,2,1,0:T(8,128)(2,1)S(1)} async-done(((bf16[16,16,16,128]{3,2,1,0:T(8,128)(2,1)}), bf16[16,16,16,128]{3,2,1,0:T(8,128)(2,1)S(1)}, u32[]{:S(2)}, u32[]{:S(2)}) %all-to-all-start.1) | async-done | bytes 1048608 | tf_op jit(solution)/shard_map/all_to_all | solution.py:509
  65.2 1.0 copy-done.5
  66.2 6.3 %shard_map.116 = bf16[16,16,16,128]{3,2,1,0:T(8,128)(2,1)} custom-call(bf16[16,16,16,128]{3,2,1,0:T(8,128)(2,1)} %copy-done.5, bf16[1024,512]{1,0:T(8,128)(2,1)} %fusion.2.go_ref.back_ref, bf16[1024,512]{1,0:T(8,128)(2,1)} %fusion.2.go_ref.back_ref, bf16[512,512]{1,0:T(8,128)(2,1)} %constant.112.clone.cosine_ref, bf16[512,512]{1,0:T(8,128)(2,1)} %constant.113.clone.sine_ref, ...), custom_call_target="tpu_custom_call" | custom-call | tf_op jit(solution)/shard_map/pallas_call | solution.py:424
  72.5 31.6 %all_to_all.25.spectra_ref = bf16[16,16,16,128]{3,2,1,0:T(8,128)(2,1)} all-to-all(bf16[16,16,16,128]{3,2,1,0:T(8,128)(2,1)} %shard_map.116), channel_id=1, replica_groups=mesh['groups'=2,'shot'=4,'rcv'=2,'rep'=2] {'shot','rcv','rep'}, dimensions={0} | all-to-all | bytes 2097152 | tf_op jit(solution)/shard_map/all_to_all | solution.py:509
  104.1 10.8 %shard_map.117 = f32[1,16,64,512]{3,2,1,0:T(8,128)} custom-call(bf16[16,16,16,128]{3,2,1,0:T(8,128)(2,1)} %all_to_all.25.spectra_ref, bf16[512,512]{1,0:T(8,128)(2,1)} %constant.109.clone.table_ref), custom_call_target="tpu_custom_call" | custom-call | tf_op jit(solution)/shard_map/pallas_call | solution.py:371
  114.9 1.7 convert_element_type.30
  116.9 2.2 copy.32
  119.1 5.4 %shard_map.118 = f32[132,16,128]{2,1,0:T(8,128)} custom-call(s32[64]{0:T(128)} %reshape.291.starts_ref, s32[64]{0:T(128)} %reshape.292.picks_ref, bf16[64,64,128]{2,1,0:T(8,128)(2,1)} %bitcast.62, bf16[8,256,128]{2,1,0:T(8,128)(2,1)} %get-tuple-element.17.tables_ref), custom_call_target="tpu_custom_call" | custom-call | tf_op jit(solution)/shard_map/pallas_call | solution.py:324
  124.5 0.9 slice.63
  125.4 2.9 %collective-permute-start.1 = (f32[3,16,128]{2,1,0:T(8,128)S(1)}, f32[3,16,128]{2,1,0:T(8,128)S(1)}, u32[]{:S(2)}, u32[]{:S(2)}) collective-permute-start(f32[3,16,128]{2,1,0:T(8,128)S(1)} %slice.63), channel_id=1, source_target_pairs={{0,1},{1,4},{4,5},{5,8},{8,9},{9,12},{12,13},{2,3},{3,6},{6,7},{7,... | collective-permute-start | bytes 73736 | tf_op jit(solution)/shard_map/ppermute | solution.py:18
  128.3 0.8 collective-permute-done.1
  129.1 1.1 fusion.6
  130.2 1.3 collective-permute-start.2
  131.5 2.5 %collective-permute-done.2 = bf16[3,16,128]{2,1,0:T(8,128)(2,1)S(1)} collective-permute-done((bf16[3,16,128]{2,1,0:T(8,128)(2,1)S(1)}, bf16[3,16,128]{2,1,0:T(8,128)(2,1)S(1)}, u32[]{:S(2)}, u32[]{:S(2)}) %collective-permute-start.2) | collective-permute-done | bytes 12320 | tf_op jit(solution)/shard_map/ppermute | solution.py:18
  134.0 1.0 maximum_maximum_fusion.1.blocks_ref
  135.0 5.4 %shard_map.119 = f32[64,64,128]{2,1,0:T(8,128)} custom-call(s32[64]{0:T(128)} %reshape.291.starts_ref, s32[64]{0:T(128)} %reshape.292.picks_ref, bf16[132,16,128]{2,1,0:T(8,128)(2,1)} %maximum_maximum_fusion.1.blocks_ref, bf16[8,256,128]{2,1,0:T(8,128)(2,1)} %get-tuple-element.16.tables_ref), custom_call_target="tpu_custom_call" | custom-call | tf_op jit(solution)/shard_map/pallas_call | solution.py:324
  140.4 3.8 %copy.47 = f32[64,4,16,128]{3,1,0,2:T(4,128)} copy(f32[64,4,16,128]{3,2,1,0:T(8,128)} %bitcast.60) | data formatting | bytes 4194304 | tf_op jit(solution)/shard_map/reshape | solution.py:503
  144.2 3.2 %reshape.298 = f32[16,64,512]{2,1,0:T(8,128)} reshape(f32[16,64,4,128]{3,2,1,0:T(4,128)} %bitcast.61) | data formatting | bytes 4194304 | tf_op jit(solution)/shard_map/reshape | solution.py:504
  147.4 2.9 %fusion.traces_ref = bf16[16,64,512]{2,1,0:T(8,128)(2,1)} fusion(f32[16,64,512]{2,1,0:T(8,128)} %reshape.298, f32[1,16,64,512]{3,2,1,0:T(8,128)S(1)} %copy-done.1), kind=kLoop, calls=%fused_computation.1 | loop fusion | flops 1048576 | bytes 5242880 | tf_op jit(solution)/shard_map/convert_element_type | solution.py:530
  150.3 11.3 %shard_map.120 = bf16[16,16,16,128]{3,2,1,0:T(8,128)(2,1)} custom-call(bf16[16,64,512]{2,1,0:T(8,128)(2,1)} %fusion.traces_ref, bf16[512,512]{1,0:T(8,128)(2,1)} %constant.109.clone.table_ref), custom_call_target="tpu_custom_call" | custom-call | tf_op jit(solution)/shard_map/pallas_call | solution.py:343
  161.6 6.2 %all-to-all-start.3 = ((bf16[16,16,16,128]{3,2,1,0:T(8,128)(2,1)}), bf16[16,16,16,128]{3,2,1,0:T(8,128)(2,1)S(1)}, u32[]{:S(2)}, u32[]{:S(2)}) async-start(bf16[16,16,16,128]{3,2,1,0:T(8,128)(2,1)} %shard_map.120), calls=%async_computation.3 | async-start | bytes 2097152 | tf_op jit(solution)/shard_map/all_to_all | solution.py:509
  167.9 0.9 broadcast_in_dim_tile.9.level_ref
  168.8 22.0 %all-to-all-done.3.spectra_ref = bf16[16,16,16,128]{3,2,1,0:T(8,128)(2,1)S(1)} async-done(((bf16[16,16,16,128]{3,2,1,0:T(8,128)(2,1)}), bf16[16,16,16,128]{3,2,1,0:T(8,128)(2,1)S(1)}, u32[]{:S(2)}, u32[]{:S(2)}) %all-to-all-start.3) | async-done | bytes 1048608 | tf_op jit(solution)/shard_map/all_to_all | solution.py:509
  190.8 1.0 copy-done.4
  191.7 5.8 %shard_map.121 = bf16[16,8,16,128]{3,2,1,0:T(8,128)(2,1)} custom-call(bf16[16,16,16,128]{3,2,1,0:T(8,128)(2,1)} %copy-done.4, bf16[1024,512]{1,0:T(8,128)(2,1)} %fusion.2.go_ref.back_ref, bf16[512,512]{1,0:T(8,128)(2,1)} %constant.111.clone.back_ref, bf16[512,512]{1,0:T(8,128)(2,1)} %constant.112.clone.cosine_ref, ...), custom_call_target="tpu_custom_call" | custom-call | tf_op jit(solution)/shard_map/pallas_call | solution.py:424
  197.5 7.2 %all-to-all-start.4 = ((bf16[16,8,16,128]{3,2,1,0:T(8,128)(2,1)}), bf16[16,8,16,128]{3,2,1,0:T(8,128)(2,1)S(1)}, u32[]{:S(2)}, u32[]{:S(2)}) async-start(bf16[16,8,16,128]{3,2,1,0:T(8,128)(2,1)} %shard_map.121), calls=%async_computation.4 | async-start | bytes 1048576 | tf_op jit(solution)/shard_map/all_to_all | solution.py:509
  204.7 1.0 copy.48
  205.8 13.2 %all-to-all-done.4.spectra_ref = bf16[16,8,16,128]{3,2,1,0:T(8,128)(2,1)S(1)} async-done(((bf16[16,8,16,128]{3,2,1,0:T(8,128)(2,1)}), bf16[16,8,16,128]{3,2,1,0:T(8,128)(2,1)S(1)}, u32[]{:S(2)}, u32[]{:S(2)}) %all-to-all-start.4) | async-done | bytes 524320 | tf_op jit(solution)/shard_map/all_to_all | solution.py:509
  219.0 0.8 copy-done.6
  219.8 6.1 %shard_map.122 = f32[2,8,32,512]{3,2,1,0:T(8,128)} custom-call(bf16[16,8,16,128]{3,2,1,0:T(8,128)(2,1)} %copy-done.6, bf16[512,512]{1,0:T(8,128)(2,1)} %constant.109.clone.table_ref), custom_call_target="tpu_custom_call" | custom-call | tf_op jit(solution)/shard_map/pallas_call | solution.py:371
  (43 shorter events, 1.6 us)
Async XLA Ops:
  0.6 7.7 %copy-start = (f32[16,16384]{1,0:T(8,128)S(1)}, f32[16,16384]{1,0:T(8,128)}, u32[]{:S(2)}) copy-start(f32[16,16384]{1,0:T(8,128)} %param.12) | copy-start | bytes 3145732
  2.0 12.0 %all-to-all-start = ((s32[8,2,1,32]{3,2,1,0:T(1,128)}), s32[8,2,1,32]{3,2,1,0:T(1,128)S(1)}, u32[]{:S(2)}, u32[]{:S(2)}) async-start(s32[8,2,1,32]{3,2,1,0:T(1,128)} %broadcast_in_dim.68), calls=%async_computation | async-start | bytes 16384 | tf_op jit(solution)/shard_map/all_to_all | solution.py:468
  8.5 7.5 %collective-permute-start = (bf16[3,16,128]{2,1,0:T(8,128)(2,1)S(1)}, bf16[3,16,128]{2,1,0:T(8,128)(2,1)S(1)}, u32[]{:S(2)}, u32[]{:S(2)}) collective-permute-start(bf16[3,16,128]{2,1,0:T(8,128)(2,1)S(1)} %slice.60), channel_id=1, source_target_pairs={{1,0},{4,1},{5,4},{8,5},{9,8},{12,9},{13,12},{3,2},{6,3},{7,6},{10... | collective-permute-start | bytes 36872 | tf_op jit(solution)/shard_map/ppermute | solution.py:18
  25.0 17.4 %copy-start.7 = (f32[2,256]{1,0:T(2,128)S(1)}, f32[2,256]{1,0:T(2,128)}, u32[]{:S(2)}) copy-start(f32[2,256]{1,0:T(2,128)} %param.16) | copy-start | bytes 6148
  25.0 19.9 %copy-start.8 = (bf16[512,512]{1,0:T(8,128)(2,1)S(1)}, bf16[512,512]{1,0:T(8,128)(2,1)}, u32[]{:S(2)}) copy-start(bf16[512,512]{1,0:T(8,128)(2,1)} %constant.110.clone) | copy-start | bytes 1572868
  36.4 28.9 %all-to-all-start.1 = ((bf16[16,16,16,128]{3,2,1,0:T(8,128)(2,1)}), bf16[16,16,16,128]{3,2,1,0:T(8,128)(2,1)S(1)}, u32[]{:S(2)}, u32[]{:S(2)}) async-start(bf16[16,16,16,128]{3,2,1,0:T(8,128)(2,1)} %shard_map.115), calls=%async_computation.1 | async-start | bytes 2097152 | tf_op jit(solution)/shard_map/all_to_all | solution.py:509
  65.2 1.0 copy-start.5
  124.5 4.6 %copy-start.2 = (f32[132,16,128]{2,1,0:T(8,128)S(1)}, f32[132,16,128]{2,1,0:T(8,128)}, u32[]{:S(2)}) copy-start(f32[132,16,128]{2,1,0:T(8,128)} %shard_map.118) | copy-start | bytes 3244036
  124.5 4.6 %slice-start = ((f32[132,16,128]{2,1,0:T(8,128)}), f32[128,16,128]{2,1,0:T(8,128)S(1)}, s32[]{:S(2)}) async-start(f32[132,16,128]{2,1,0:T(8,128)} %shard_map.118), calls=%async_computation.5 | async-start | bytes 2097152 | tf_op jit(solution)/shard_map/slice | solution.py:527
  125.4 3.7 %collective-permute-start.1 = (f32[3,16,128]{2,1,0:T(8,128)S(1)}, f32[3,16,128]{2,1,0:T(8,128)S(1)}, u32[]{:S(2)}, u32[]{:S(2)}) collective-permute-start(f32[3,16,128]{2,1,0:T(8,128)S(1)} %slice.63), channel_id=1, source_target_pairs={{0,1},{1,4},{4,5},{5,8},{8,9},{9,12},{12,13},{2,3},{3,6},{6,7},{7,... | collective-permute-start | bytes 73736 | tf_op jit(solution)/shard_map/ppermute | solution.py:18
  130.2 3.7 %collective-permute-start.2 = (bf16[3,16,128]{2,1,0:T(8,128)(2,1)S(1)}, bf16[3,16,128]{2,1,0:T(8,128)(2,1)S(1)}, u32[]{:S(2)}, u32[]{:S(2)}) collective-permute-start(bf16[3,16,128]{2,1,0:T(8,128)(2,1)S(1)} %slice.64), channel_id=1, source_target_pairs={{1,0},{4,1},{5,4},{8,5},{9,8},{12,9},{13,12},{3,2},{6,3},{7,6},{10... | collective-permute-start | bytes 36872 | tf_op jit(solution)/shard_map/ppermute | solution.py:18
  144.2 3.2 %copy-start.1 = (f32[1,16,64,512]{3,2,1,0:T(8,128)S(1)}, f32[1,16,64,512]{3,2,1,0:T(8,128)}, u32[]{:S(2)}) copy-start(f32[1,16,64,512]{3,2,1,0:T(8,128)} %shard_map.117) | copy-start | bytes 6291460
  161.6 29.1 %all-to-all-start.3 = ((bf16[16,16,16,128]{3,2,1,0:T(8,128)(2,1)}), bf16[16,16,16,128]{3,2,1,0:T(8,128)(2,1)S(1)}, u32[]{:S(2)}, u32[]{:S(2)}) async-start(bf16[16,16,16,128]{3,2,1,0:T(8,128)(2,1)} %shard_map.120), calls=%async_computation.3 | async-start | bytes 2097152 | tf_op jit(solution)/shard_map/all_to_all | solution.py:509
  168.8 36.0 %copy-start.3 = (f32[128,2,8,128]{3,2,1,0:T(8,128)S(1)}, f32[128,2,8,128]{3,2,1,0:T(8,128)}, u32[]{:S(2)}) copy-start(f32[128,2,8,128]{3,2,1,0:T(8,128)} %get-tuple-element.22) | copy-start | bytes 3145732
  190.8 1.0 copy-start.4
  197.5 21.5 %all-to-all-start.4 = ((bf16[16,8,16,128]{3,2,1,0:T(8,128)(2,1)}), bf16[16,8,16,128]{3,2,1,0:T(8,128)(2,1)S(1)}, u32[]{:S(2)}, u32[]{:S(2)}) async-start(bf16[16,8,16,128]{3,2,1,0:T(8,128)(2,1)} %shard_map.121), calls=%async_computation.4 | async-start | bytes 1048576 | tf_op jit(solution)/shard_map/all_to_all | solution.py:509
  219.0 0.8 copy-start.6
where the time goes:
time: 229 us; the launch traced here: 226 us
  Pallas kernels  69.4 us (30%)
  waiting for transfers between devices  58.1 us (25%)
  blocking collectives  31.6 us (14%)
  starting transfers between devices  31.2 us (14%)
  local copies, waits for them, and re-layouts  21.2 us (9%)
  other arithmetic  11.8 us (5%)
    all_to_all x3, waiting for transfers between devices, swap(): return lax.all_to_all(value, everyone, 0, 0, tiled=True)  53.8 us
    all_to_all x1, blocking collectives, swap(): return lax.all_to_all(value, everyone, 0, 0, tiled=True)  31.6 us
    pallas_call x2, Pallas kernels, spectrum(): pl.pallas_call(spectrum_kernel, grid=(rcv,), out_shape=jax.ShapeDtypeStru...  22.7 us
    all_to_all x3, starting transfers between devices, swap(): return lax.all_to_all(value, everyone, 0, 0, tiled=True)  19.4 us
    pallas_call x2, Pallas kernels, records_of(): pl.pallas_call(record_kernel, grid=(rcv,), out_shape=jax.ShapeDtypeStruct...  16.9 us
    pallas_call x3, Pallas kernels, slot_call(): pl.pallas_call(kernel, out_shape=out_shape, in_specs=[smem, smem, vmem, v...  15.9 us
    pallas_call x2, Pallas kernels, bins_stage(): pl.pallas_call(functools.partial(bins_kernel, place, halves), out_shape=j...  12.1 us
    all_to_all x1, starting transfers between devices, body_by_slots(): lax.all_to_all(jnp.broadcast_to(shots[None], (slab_count,) + shots.shape)...  6.35 us
  transfers between devices with their start and end apart: 7, of which 6 were waited for; matrix products, arithmetic and copies ran while one was open for 4% of the time, Pallas kernels for 1%

commit v1 on v0

--- a/solution.py
+++ b/solution.py
@@ -285,98 +285,152 @@
     return table.astype(jnp.bfloat16).astype(np.float32)
 
 
-def correlate_kernel(starts_ref, picks_ref, blocks_ref, tables_ref, out_ref):
-    slots, rows, taps = out_ref.shape
-    rcv = blocks_ref.shape[1]
+def analyse(with_model, starts_ref, picks_ref, blocks_ref, taps_ref, table_ref, *rest):
+    model_ref = rest[0] if with_model else None
+    out_ref, held_ref = rest[-2:]
+    rcv, taps = blocks_ref.shape[1:]
+    parts, _, bins, lanes = out_ref.shape
+    slots = lanes // 2
+    rows = held_ref.shape[0] // slots
     steps = rows // rcv
+    half = parts * bins
 
     def one(slot, carry):
         window = blocks_ref[pl.ds(starts_ref[slot], steps)].reshape(rows, taps)
         later = jnp.concatenate([window[rcv:], jnp.zeros((rcv, taps), window.dtype)], axis=0)
         pair = jnp.concatenate([window, later], axis=1)
-        out_ref[slot] = dot(pair, tables_ref[picks_ref[slot]]).astype(out_ref.dtype)
+        terms = dot(pair, taps_ref[picks_ref[slot]])
+        where = pl.ds(pl.multiple_of(slot * rows, rows), rows)
+        if with_model:
+            terms = terms + model_ref[where]
+        held_ref[where] = terms
         return carry
 
-    lax.fori_loop(0, slots, one, 0, unroll=4)
-
-
-def blend_kernel(starts_ref, picks_ref, traces_ref, tables_ref, out_ref):
-    slots, rows, taps = traces_ref.shape
-    rcv = out_ref.shape[1]
+    lax.fori_loop(0, slots, one, 0, unroll=8)
+    together = math.gcd(rcv, 4)
+    for first in range(0, rcv, together):
+        traces = jnp.concatenate(
+            [
+                jnp.concatenate(
+                    [
+                        held_ref[pl.ds(step * rcv + line, slots, stride=rows), :].astype(jnp.bfloat16)
+                        for step in range(steps)
+                    ],
+                    axis=1,
+                )
+                for line in range(first, first + together)
+            ],
+            axis=0,
+        )
+        both = dot(table_ref[...], traces, 1, 1)
+        for line in range(together):
+            piece = both[:, line * slots : (line + 1) * slots]
+            joined = jnp.concatenate([piece[:half], piece[half:]], axis=1)
+            out_ref[:, first + line] = joined.reshape(parts, bins, lanes).astype(jnp.bfloat16)
+
+
+def slots_to_spectra(starts, picks, blocks, taps, table, model, parts, slots):
+    rcv, width = blocks.shape[1:]
+    samples = table.shape[1]
+    vmem = pl.BlockSpec(memory_space=pltpu.VMEM)
+    smem = pl.BlockSpec(memory_space=pltpu.SMEM)
+    extra = () if model is None else (model,)
+    return pl.pallas_call(
+        functools.partial(analyse, model is not None),
+        out_shape=jax.ShapeDtypeStruct((parts, rcv, samples // 2 // parts, 2 * slots), jnp.bfloat16),
+        in_specs=[smem, smem, vmem, vmem, vmem] + [vmem] * len(extra),
+        out_specs=vmem,
+        scratch_shapes=[pltpu.VMEM((slots * rcv * samples // width, width), jnp.float32)],
+    )(starts, picks, blocks, taps, table, *extra)
+
+
+def upright(spectra_ref, lines, group_lanes):
+    parts, _, bins, _ = spectra_ref.shape
+    pieces = []
+    for line in lines:
+        turned = spectra_ref[:, line].reshape(parts * bins, -1).astype(jnp.float32).T
+        turned = turned.astype(jnp.bfloat16)
+        count = group_lanes // 2
+        for low in range(0, turned.shape[0], group_lanes):
+            pieces.append(
+                jnp.concatenate(
+                    [turned[low : low + count], turned[low + count : low + 2 * count]], axis=1
+                )
+            )
+    return jnp.concatenate(pieces, axis=0)
+
+
+def synthesise(starts_ref, picks_ref, spectra_ref, taps_ref, table_ref, model_ref, total_ref):
+    rcv, lanes = spectra_ref.shape[1], spectra_ref.shape[3]
+    slots = lanes // 2
+    taps = model_ref.shape[1]
+    rows = model_ref.shape[0] // slots
     steps = rows // rcv
-    out_ref[...] = jnp.zeros_like(out_ref)
+    together = math.gcd(rcv, 4)
+    for first in range(0, rcv, together):
+        lines = range(first, first + together)
+        fields = dot(upright(spectra_ref, lines, lanes), table_ref[...])
+        for line in lines:
+            low = (line - first) * slots
+            for step in range(steps):
+                model_ref[pl.ds(step * rcv + line, slots, stride=rows), :] = fields[
+                    low : low + slots, step * taps : (step + 1) * taps
+                ]
+    total_ref[...] = jnp.zeros_like(total_ref)
 
     def one(slot, carry):
-        trace = traces_ref[slot]
+        trace = model_ref[pl.ds(pl.multiple_of(slot * rows, rows), rows)].astype(jnp.bfloat16)
         earlier = jnp.concatenate([jnp.zeros((rcv, taps), trace.dtype), trace[:-rcv]], axis=0)
         pair = jnp.concatenate([trace, earlier], axis=1)
-        shot = dot(pair, tables_ref[picks_ref[slot]]).astype(jnp.bfloat16).astype(jnp.float32)
+        shot = dot(pair, taps_ref[picks_ref[slot]]).astype(jnp.bfloat16).astype(jnp.float32)
         where = pl.ds(starts_ref[slot], steps)
-        out_ref[where] = out_ref[where] + shot.reshape(steps, rcv, taps)
+        total_ref[where] = total_ref[where] + shot.reshape(steps, rcv, taps)
         return carry
 
-    lax.fori_loop(0, slots, one, 0, unroll=4)
-
-
-def slot_call(kernel, out_shape, starts, picks, data, tables):
+    lax.fori_loop(0, slots, one, 0, unroll=8)
+
+
+def spectra_to_slab(starts, picks, spectra, taps, table, slab_blocks):
+    _, rcv, _, lanes = spectra.shape
+    width = taps.shape[2]
+    steps = table.shape[1] // width
     vmem = pl.BlockSpec(memory_space=pltpu.VMEM)
     smem = pl.BlockSpec(memory_space=pltpu.SMEM)
     return pl.pallas_call(
-        kernel,
-        out_shape=out_shape,
-        in_specs=[smem, smem, vmem, vmem],
-        out_specs=vmem,
-    )(starts, picks, data, tables)
-
-
-def spectrum_kernel(traces_ref, table_ref, out_ref):
-    parts, _, bins, _ = out_ref.shape
-    both = dot(table_ref[...], traces_ref[0], 1, 1)
-    half = parts * bins
-    joined = jnp.concatenate([both[:half], both[half:]], axis=1)
-    out_ref[:, 0] = joined.reshape(parts, bins, joined.shape[1]).astype(jnp.bfloat16)
-
-
-def spectrum(traces, table, parts):
-    rcv, slots, samples = traces.shape
-    bins = samples // 2 // parts
-    return pl.pallas_call(
-        spectrum_kernel,
-        grid=(rcv,),
-        out_shape=jax.ShapeDtypeStruct((parts, rcv, bins, 2 * slots), jnp.bfloat16),
-        in_specs=[
-            pl.BlockSpec((1, slots, samples), lambda i: (i, 0, 0)),
-            pl.BlockSpec((samples, samples), lambda i: (0, 0)),
-        ],
-        out_specs=pl.BlockSpec((parts, 1, bins, 2 * slots), lambda i: (0, i, 0, 0)),
-    )(traces, table)
-
-
-def record_kernel(spectra_ref, table_ref, out_ref):
-    parts, _, bins, lanes = spectra_ref.shape
-    half = parts * bins
-    groups, _, count, _ = out_ref.shape
-    values = spectra_ref[:, 0].reshape(half, lanes)
-    first = dot(values, table_ref[:half], 0, 0)
-    second = dot(values, table_ref[half:], 0, 0)
-    for group in range(groups):
-        low = 2 * group * count
-        out_ref[group, 0] = first[low : low + count] + second[low + count : low + 2 * count]
+        synthesise,
+        out_shape=(
+            jax.ShapeDtypeStruct((lanes // 2 * rcv * steps, width), jnp.float32),
+            jax.ShapeDtypeStruct((slab_blocks + steps, rcv, width), jnp.float32),
+        ),
+        in_specs=[smem, smem, vmem, vmem, vmem],
+        out_specs=(vmem, vmem),
+    )(starts, picks, spectra, taps, table)
+
+
+def record_kernel(groups, spectra_ref, table_ref, out_ref):
+    count = out_ref.shape[2]
+    together = spectra_ref.shape[1]
+    fields = dot(upright(spectra_ref, range(together), 2 * count), table_ref[...])
+    for line in range(together):
+        for group in range(groups):
+            low = (line * groups + group) * count
+            out_ref[group, line] = fields[low : low + count]
 
 
 def records_of(spectra, table, groups):
     parts, rcv, bins, lanes = spectra.shape
     samples = table.shape[1]
     count = lanes // 2 // groups
+    together = math.gcd(rcv, 4)
     return pl.pallas_call(
-        record_kernel,
-        grid=(rcv,),
+        functools.partial(record_kernel, groups),
+        grid=(rcv // together,),
         out_shape=jax.ShapeDtypeStruct((groups, rcv, count, samples), jnp.float32),
         in_specs=[
-            pl.BlockSpec((parts, 1, bins, lanes), lambda i: (0, i, 0, 0)),
+            pl.BlockSpec((parts, together, bins, lanes), lambda i: (0, i, 0, 0)),
             pl.BlockSpec((samples, samples), lambda i: (0, 0)),
         ],
-        out_specs=pl.BlockSpec((groups, 1, count, samples), lambda i: (0, i, 0, 0)),
+        out_specs=pl.BlockSpec((groups, together, count, samples), lambda i: (0, i, 0, 0)),
     )(spectra, table)
 
 
@@ -494,41 +548,37 @@
     picks = jnp.sum(jnp.where(mine, every_pick[:, None, :], 0), axis=2).reshape(-1)
     forward_tables, adjoint_tables = toeplitz_tables(signatures)
 
-    def correlate(blocks, dtype):
+    def correlate(blocks, model):
         low = blocks.astype(jnp.bfloat16)
         rim = from_behind(low[: steps - 1], ("shot", "rep"), -1)
         extended = jnp.concatenate([low, rim, jnp.zeros_like(low[:1])], axis=0)
-        shape = jax.ShapeDtypeStruct((slots, steps * local_rcv, tap_count), dtype)
-        terms = slot_call(correlate_kernel, shape, starts, picks, extended, adjoint_tables)
-        terms = terms.reshape(slots, steps, local_rcv, tap_count).transpose(2, 0, 1, 3)
-        return terms.reshape(local_rcv, slots, NT)
+        return slots_to_spectra(
+            starts, picks, extended, adjoint_tables, time_table_fixed, model, parts, slots
+        )
 
     bin_start = lax.axis_index(everyone) * bins
 
     def swap(value):
         return lax.all_to_all(value, everyone, 0, 0, tiled=True)
 
-    def shrink_at(traces, index, back, halves):
+    def shrink_at(spectra, index, back, halves):
         level = lax.dynamic_slice_in_dim(thresholds[index], bin_start, bins)
         level = jnp.tile(level, local_rcv * rcv_count)[:, None]
-        spectra = swap(spectrum(traces, time_table_fixed, parts))
-        spectra = swap(
-            bins_stage(spectra, slot_table, back, cosine, sine, level, place, halves)
-        )
-        return records_of(spectra, time_table_fixed, halves)
+        return swap(
+            bins_stage(swap(spectra), slot_table, back, cosine, sine, level, place, halves)
+        )
 
     record_blocks = records.reshape(local_rcv, slab_blocks, tap_count).transpose(1, 0, 2)
-    model = shrink_at(correlate(record_blocks, jnp.bfloat16), 0, slot_table, 1)[0]
-    traces = model.astype(jnp.bfloat16).reshape(local_rcv, slots, steps, tap_count)
-    traces = traces.transpose(1, 2, 0, 3).reshape(slots, steps * local_rcv, tap_count)
-    shape = jax.ShapeDtypeStruct((slab_blocks + steps, local_rcv, tap_count), jnp.float32)
-    total = slot_call(blend_kernel, shape, starts, picks, traces, forward_tables)
+    spectra = shrink_at(correlate(record_blocks, None), 0, slot_table, 1)
+    model, total = spectra_to_slab(
+        starts, picks, spectra, forward_tables, time_table_fixed, slab_blocks
+    )
     carried = from_behind(total[slab_blocks : slab_blocks + steps - 1], ("shot", "rep"), 1)
     blended = total[:slab_blocks].at[: steps - 1].add(carried)
     left = record_blocks - blended
     residual = left.transpose(1, 0, 2).reshape(local_rcv, slab_len)
-    traces = (model + correlate(left, jnp.float32)).astype(jnp.bfloat16)
-    model = shrink_at(traces, 1, row_table, 2)
+    spectra = shrink_at(correlate(left, model), 1, row_table, 2)
+    model = records_of(spectra, time_table_fixed, 2)
     return (model.reshape(rows_here, local_rcv, shot_count, NT), residual)
 
 

time: 229 us -> 176 us (0.77)
  Pallas kernels: 69.4 us -> 36 us
  local copies, waits for them, and re-layouts: 21.2 us -> 9.96 us
  other arithmetic: 11.8 us -> 6.92 us
    pallas_call x7 -> x4, Pallas kernels: 55.4 us -> 22.1 us  [the longest x2 12.2 us: slots_to_spectra(): pl.pallas_call(functools.partial(analyse, model is not None), out_shape=j...]
    reshape x4 -> x0, local copies, waits for them, and re-layouts: 9.93 us -> none  [the longest x2 5.49 us: correlate(): terms.reshape(slots, steps, local_rcv, tap_count).transpose(2, 0, 1, 3)]
    convert_element_type x2 -> x0, other arithmetic: 4.64 us -> none  [the longest x1 2.91 us: body_by_slots(): traces = (model + correlate(left, jnp.float32)).astype(jnp.bfloat16)]
    convert_element_type x2 -> x0, local copies, waits for them, and re-layouts: 2.48 us -> none  [body_by_slots(): model.astype(jnp.bfloat16).reshape(local_rcv, slots, steps, tap_count)]
  transfers between devices with their start and end apart: 7 -> 7, of which waited for: 6 -> 5; matrix products, arithmetic and copies ran while one was open for 4% -> 6% of each run, Pallas kernels for 1% -> 1%
where the time goes in v1:
time: 176 us; the launch traced here: 175 us
  waiting for transfers between devices  57.2 us (32%)
  Pallas kernels  36 us (20%)
  blocking collectives  31.6 us (18%)
  starting transfers between devices  30.9 us (18%)
  local copies, waits for them, and re-layouts  9.96 us (6%)
  other arithmetic  6.92 us (4%)
    all_to_all x3, waiting for transfers between devices, swap(): return lax.all_to_all(value, everyone, 0, 0, tiled=True)  53.8 us
    all_to_all x1, blocking collectives, swap(): return lax.all_to_all(value, everyone, 0, 0, tiled=True)  31.6 us
    all_to_all x3, starting transfers between devices, swap(): return lax.all_to_all(value, everyone, 0, 0, tiled=True)  19.1 us
    pallas_call x2, Pallas kernels, slots_to_spectra(): pl.pallas_call(functools.partial(analyse, model is not None), out_shape=j...  12.2 us
    pallas_call x2, Pallas kernels, bins_stage(): pl.pallas_call(functools.partial(bins_kernel, place, halves), out_shape=j...  12.1 us
    pallas_call x1, Pallas kernels, spectra_to_slab(): pl.pallas_call(synthesise, out_shape=(jax.ShapeDtypeStruct((lanes // 2 *...  7.17 us
    all_to_all x1, starting transfers between devices, body_by_slots(): lax.all_to_all(jnp.broadcast_to(shots[None], (slab_count,) + shots.shape)...  6.35 us
    ppermute x3, starting transfers between devices, from_behind(): lax.ppermute(value, axis, [(source, source + steps) for source in range(f...  5.44 us
  transfers between devices with their start and end apart: 7, of which 5 were waited for; matrix products, arithmetic and copies ran while one was open for 6% of the time, Pallas kernels for 1%

profile of v1, /device:TPU:0, one launch (start us, length us, event | category | flops | bytes accessed | tf_op | source)
XLA Modules:
  0.0 175.1 jit_solution(16029490132034213397)
XLA Ops:
  0.6 0.8 pad_add_fusion
  1.4 0.6 broadcast_in_dim.68
  2.0 6.4 %all-to-all-start = ((s32[8,2,1,32]{3,2,1,0:T(1,128)}), s32[8,2,1,32]{3,2,1,0:T(1,128)S(1)}, u32[]{:S(2)}, u32[]{:S(2)}) async-start(s32[8,2,1,32]{3,2,1,0:T(1,128)} %broadcast_in_dim.68), calls=%async_computation | async-start | bytes 16384 | tf_op jit(solution)/shard_map/all_to_all | solution.py:522
  8.4 0.1 fusion.3
  8.5 1.3 collective-permute-start
  9.8 1.3 convert_element_type.18.taps_ref
  11.1 1.8 %shard_map.113 = (bf16[8,256,128]{2,1,0:T(8,128)(2,1)}, bf16[8,256,128]{2,1,0:T(8,128)(2,1)}) custom-call(f32[8,128]{1,0:T(8,128)} %convert_element_type.18.taps_ref), custom_call_target="tpu_custom_call" | custom-call | tf_op jit(solution)/shard_map/pallas_call | solution.py:72
  12.9 0.1 pad.7.clone
  13.0 1.0 all-to-all-done
  14.0 0.3 convert_reduce_fusion
  14.3 0.4 select_reduce_fusion.1
  14.7 0.7 reshape.273.starts_ref
  15.3 0.6 reshape.274.picks_ref
  15.9 1.0 maximum_maximum_fusion.blocks_ref
  17.0 5.8 %shard_map.114 = bf16[16,16,16,128]{3,2,1,0:T(8,128)(2,1)} custom-call(s32[64]{0:T(128)} %reshape.273.starts_ref, s32[64]{0:T(128)} %reshape.274.picks_ref, bf16[132,16,128]{2,1,0:T(8,128)(2,1)} %maximum_maximum_fusion.blocks_ref, bf16[8,256,128]{2,1,0:T(8,128)(2,1)} %get-tuple-element.18.taps_ref, bf16[512,512]{1,0:T(8,128)(2,1)} %constant.109.clone.table_ref), custom_call_target="tpu_custom_call" | custom-call | tf_op jit(solution)/shard_map/pallas_call | solution.py:338
  22.7 6.0 %all-to-all-start.1 = ((bf16[16,16,16,128]{3,2,1,0:T(8,128)(2,1)}), bf16[16,16,16,128]{3,2,1,0:T(8,128)(2,1)S(1)}, u32[]{:S(2)}, u32[]{:S(2)}) async-start(bf16[16,16,16,128]{3,2,1,0:T(8,128)(2,1)} %shard_map.114), calls=%async_computation.1 | async-start | bytes 2097152 | tf_op jit(solution)/shard_map/all_to_all | solution.py:562
  28.8 0.1 fusion.12
  28.9 0.9 broadcast_in_dim_tile.8.level_ref
  29.8 1.2 select_reduce_fusion
  31.0 0.1 sub.22
  31.1 0.1 gt.16
  31.2 0.1 add_select_fusion
  31.2 0.1 select_n.71
  31.3 1.7 fusion.1.go_ref.back_ref
  33.0 18.6 %all-to-all-done.1.spectra_ref = bf16[16,16,16,128]{3,2,1,0:T(8,128)(2,1)S(1)} async-done(((bf16[16,16,16,128]{3,2,1,0:T(8,128)(2,1)}), bf16[16,16,16,128]{3,2,1,0:T(8,128)(2,1)S(1)}, u32[]{:S(2)}, u32[]{:S(2)}) %all-to-all-start.1) | async-done | bytes 1048608 | tf_op jit(solution)/shard_map/all_to_all | solution.py:562
  51.7 1.0 copy-done.2
  52.6 6.3 %shard_map.115 = bf16[16,16,16,128]{3,2,1,0:T(8,128)(2,1)} custom-call(bf16[16,16,16,128]{3,2,1,0:T(8,128)(2,1)} %copy-done.2, bf16[1024,512]{1,0:T(8,128)(2,1)} %fusion.1.go_ref.back_ref, bf16[1024,512]{1,0:T(8,128)(2,1)} %fusion.1.go_ref.back_ref, bf16[512,512]{1,0:T(8,128)(2,1)} %constant.112.clone.cosine_ref, bf16[512,512]{1,0:T(8,128)(2,1)} %constant.113.clone.sine_ref, ...), custom_call_target="tpu_custom_call" | custom-call | tf_op jit(solution)/shard_map/pallas_call | solution.py:478
  58.9 31.6 %all_to_all.25.spectra_ref = bf16[16,16,16,128]{3,2,1,0:T(8,128)(2,1)} all-to-all(bf16[16,16,16,128]{3,2,1,0:T(8,128)(2,1)} %shard_map.115), channel_id=1, replica_groups=mesh['groups'=2,'shot'=4,'rcv'=2,'rep'=2] {'shot','rcv','rep'}, dimensions={0} | all-to-all | bytes 2097152 | tf_op jit(solution)/shard_map/all_to_all | solution.py:562
  90.5 7.2 %shard_map.116 = (f32[4096,128]{1,0:T(8,128)}, f32[132,16,128]{2,1,0:T(8,128)}) custom-call(s32[64]{0:T(128)} %reshape.273.starts_ref, s32[64]{0:T(128)} %reshape.274.picks_ref, bf16[16,16,16,128]{3,2,1,0:T(8,128)(2,1)} %all_to_all.25.spectra_ref, bf16[8,256,128]{2,1,0:T(8,128)(2,1)} %get-tuple-element.19.taps_ref, bf16[512,512]{1,0:T(8,128)(2,1)} %constant.109.clone.table_ref), custom_call_target="tpu_custom_call" | custom-call | tf_op jit(solution)/shard_map/pallas_call | solution.py:399
  97.7 0.7 slice.55
  98.4 2.9 %collective-permute-start.1 = (f32[3,16,128]{2,1,0:T(8,128)S(1)}, f32[3,16,128]{2,1,0:T(8,128)S(1)}, u32[]{:S(2)}, u32[]{:S(2)}) collective-permute-start(f32[3,16,128]{2,1,0:T(8,128)S(1)} %slice.55), channel_id=1, source_target_pairs={{0,1},{1,4},{4,5},{5,8},{8,9},{9,12},{12,13},{2,3},{3,6},{6,7},{7,... | collective-permute-start | bytes 73736 | tf_op jit(solution)/shard_map/ppermute | solution.py:18
  101.3 1.3 slice.53
  102.6 0.7 add_dynamic-update-slice_fusion
  103.3 0.1 fusion.5
  103.5 1.3 collective-permute-start.2
  104.8 2.4 %collective-permute-done.2 = bf16[3,16,128]{2,1,0:T(8,128)(2,1)S(1)} collective-permute-done((bf16[3,16,128]{2,1,0:T(8,128)(2,1)S(1)}, bf16[3,16,128]{2,1,0:T(8,128)(2,1)S(1)}, u32[]{:S(2)}, u32[]{:S(2)}) %collective-permute-start.2) | collective-permute-done | bytes 12320 | tf_op jit(solution)/shard_map/ppermute | solution.py:18
  107.1 1.0 maximum_maximum_fusion.1.blocks_ref
  108.2 6.5 %shard_map.117 = bf16[16,16,16,128]{3,2,1,0:T(8,128)(2,1)} custom-call(s32[64]{0:T(128)} %reshape.273.starts_ref, s32[64]{0:T(128)} %reshape.274.picks_ref, bf16[132,16,128]{2,1,0:T(8,128)(2,1)} %maximum_maximum_fusion.1.blocks_ref, bf16[8,256,128]{2,1,0:T(8,128)(2,1)} %get-tuple-element.18.taps_ref, bf16[512,512]{1,0:T(8,128)(2,1)} %constant.109.clone.table_ref, ...), custom_call_target="tpu_custom_call" | custom-call | tf_op jit(solution)/shard_map/pallas_call | solution.py:338
  114.6 5.9 %all-to-all-start.3 = ((bf16[16,16,16,128]{3,2,1,0:T(8,128)(2,1)}), bf16[16,16,16,128]{3,2,1,0:T(8,128)(2,1)S(1)}, u32[]{:S(2)}, u32[]{:S(2)}) async-start(bf16[16,16,16,128]{3,2,1,0:T(8,128)(2,1)} %shard_map.117), calls=%async_computation.3 | async-start | bytes 2097152 | tf_op jit(solution)/shard_map/all_to_all | solution.py:562
  120.5 0.9 broadcast_in_dim_tile.9.level_ref
  121.4 22.0 %all-to-all-done.3.spectra_ref = bf16[16,16,16,128]{3,2,1,0:T(8,128)(2,1)S(1)} async-done(((bf16[16,16,16,128]{3,2,1,0:T(8,128)(2,1)}), bf16[16,16,16,128]{3,2,1,0:T(8,128)(2,1)S(1)}, u32[]{:S(2)}, u32[]{:S(2)}) %all-to-all-start.3) | async-done | bytes 1048608 | tf_op jit(solution)/shard_map/all_to_all | solution.py:562
  143.4 1.0 copy-done.1
  144.4 5.8 %shard_map.118 = bf16[16,8,16,128]{3,2,1,0:T(8,128)(2,1)} custom-call(bf16[16,16,16,128]{3,2,1,0:T(8,128)(2,1)} %copy-done.1, bf16[1024,512]{1,0:T(8,128)(2,1)} %fusion.1.go_ref.back_ref, bf16[512,512]{1,0:T(8,128)(2,1)} %constant.111.clone.back_ref, bf16[512,512]{1,0:T(8,128)(2,1)} %constant.112.clone.cosine_ref, ...), custom_call_target="tpu_custom_call" | custom-call | tf_op jit(solution)/shard_map/pallas_call | solution.py:478
  150.1 7.2 %all-to-all-start.4 = ((bf16[16,8,16,128]{3,2,1,0:T(8,128)(2,1)}), bf16[16,8,16,128]{3,2,1,0:T(8,128)(2,1)S(1)}, u32[]{:S(2)}, u32[]{:S(2)}) async-start(bf16[16,8,16,128]{3,2,1,0:T(8,128)(2,1)} %shard_map.118), calls=%async_computation.4 | async-start | bytes 1048576 | tf_op jit(solution)/shard_map/all_to_all | solution.py:562
  157.3 1.0 copy.33
  158.4 13.2 %all-to-all-done.4.spectra_ref = bf16[16,8,16,128]{3,2,1,0:T(8,128)(2,1)S(1)} async-done(((bf16[16,8,16,128]{3,2,1,0:T(8,128)(2,1)}), bf16[16,8,16,128]{3,2,1,0:T(8,128)(2,1)S(1)}, u32[]{:S(2)}, u32[]{:S(2)}) %all-to-all-start.4) | async-done | bytes 524320 | tf_op jit(solution)/shard_map/all_to_all | solution.py:562
  171.6 0.8 copy-done.3
  172.4 2.7 %shard_map.119 = f32[2,8,32,512]{3,2,1,0:T(8,128)} custom-call(bf16[16,8,16,128]{3,2,1,0:T(8,128)(2,1)} %copy-done.3, bf16[512,512]{1,0:T(8,128)(2,1)} %constant.109.clone.table_ref), custom_call_target="tpu_custom_call" | custom-call | tf_op jit(solution)/shard_map/pallas_call | solution.py:425
  (25 shorter events, 0.1 us)
Async XLA Ops:
  0.6 7.7 %copy-start = (f32[16,16384]{1,0:T(8,128)S(1)}, f32[16,16384]{1,0:T(8,128)}, u32[]{:S(2)}) copy-start(f32[16,16384]{1,0:T(8,128)} %param.12) | copy-start | bytes 3145732
  2.0 12.0 %all-to-all-start = ((s32[8,2,1,32]{3,2,1,0:T(1,128)}), s32[8,2,1,32]{3,2,1,0:T(1,128)S(1)}, u32[]{:S(2)}, u32[]{:S(2)}) async-start(s32[8,2,1,32]{3,2,1,0:T(1,128)} %broadcast_in_dim.68), calls=%async_computation | async-start | bytes 16384 | tf_op jit(solution)/shard_map/all_to_all | solution.py:522
  8.5 7.5 %collective-permute-start = (bf16[3,16,128]{2,1,0:T(8,128)(2,1)S(1)}, bf16[3,16,128]{2,1,0:T(8,128)(2,1)S(1)}, u32[]{:S(2)}, u32[]{:S(2)}) collective-permute-start(bf16[3,16,128]{2,1,0:T(8,128)(2,1)S(1)} %slice.60), channel_id=1, source_target_pairs={{1,0},{4,1},{5,4},{8,5},{9,8},{12,9},{13,12},{3,2},{6,3},{7,6},{10... | collective-permute-start | bytes 36872 | tf_op jit(solution)/shard_map/ppermute | solution.py:18
  17.0 11.8 %copy-start.4 = (f32[2,256]{1,0:T(2,128)S(1)}, f32[2,256]{1,0:T(2,128)}, u32[]{:S(2)}) copy-start(f32[2,256]{1,0:T(2,128)} %param.16) | copy-start | bytes 6148
  17.0 14.4 %copy-start.5 = (bf16[512,512]{1,0:T(8,128)(2,1)S(1)}, bf16[512,512]{1,0:T(8,128)(2,1)}, u32[]{:S(2)}) copy-start(bf16[512,512]{1,0:T(8,128)(2,1)} %constant.110.clone) | copy-start | bytes 1572868
  22.7 28.9 %all-to-all-start.1 = ((bf16[16,16,16,128]{3,2,1,0:T(8,128)(2,1)}), bf16[16,16,16,128]{3,2,1,0:T(8,128)(2,1)S(1)}, u32[]{:S(2)}, u32[]{:S(2)}) async-start(bf16[16,16,16,128]{3,2,1,0:T(8,128)(2,1)} %shard_map.114), calls=%async_computation.1 | async-start | bytes 2097152 | tf_op jit(solution)/shard_map/all_to_all | solution.py:562
  51.7 1.0 copy-start.2
  98.4 4.2 %collective-permute-start.1 = (f32[3,16,128]{2,1,0:T(8,128)S(1)}, f32[3,16,128]{2,1,0:T(8,128)S(1)}, u32[]{:S(2)}, u32[]{:S(2)}) collective-permute-start(f32[3,16,128]{2,1,0:T(8,128)S(1)} %slice.55), channel_id=1, source_target_pairs={{0,1},{1,4},{4,5},{5,8},{8,9},{9,12},{12,13},{2,3},{3,6},{6,7},{7,... | collective-permute-start | bytes 73736 | tf_op jit(solution)/shard_map/ppermute | solution.py:18
  103.5 3.7 %collective-permute-start.2 = (bf16[3,16,128]{2,1,0:T(8,128)(2,1)S(1)}, bf16[3,16,128]{2,1,0:T(8,128)(2,1)S(1)}, u32[]{:S(2)}, u32[]{:S(2)}) collective-permute-start(bf16[3,16,128]{2,1,0:T(8,128)(2,1)S(1)} %slice.61), channel_id=1, source_target_pairs={{1,0},{4,1},{5,4},{8,5},{9,8},{12,9},{13,12},{3,2},{6,3},{7,6},{10... | collective-permute-start | bytes 36872 | tf_op jit(solution)/shard_map/ppermute | solution.py:18
  114.6 28.8 %all-to-all-start.3 = ((bf16[16,16,16,128]{3,2,1,0:T(8,128)(2,1)}), bf16[16,16,16,128]{3,2,1,0:T(8,128)(2,1)S(1)}, u32[]{:S(2)}, u32[]{:S(2)}) async-start(bf16[16,16,16,128]{3,2,1,0:T(8,128)(2,1)} %shard_map.117), calls=%async_computation.3 | async-start | bytes 2097152 | tf_op jit(solution)/shard_map/all_to_all | solution.py:562
  143.4 1.0 copy-start.1
  150.1 21.5 %all-to-all-start.4 = ((bf16[16,8,16,128]{3,2,1,0:T(8,128)(2,1)}), bf16[16,8,16,128]{3,2,1,0:T(8,128)(2,1)S(1)}, u32[]{:S(2)}, u32[]{:S(2)}) async-start(bf16[16,8,16,128]{3,2,1,0:T(8,128)(2,1)} %shard_map.118), calls=%async_computation.4 | async-start | bytes 1048576 | tf_op jit(solution)/shard_map/all_to_all | solution.py:562
  171.6 0.8 copy-start.3

commit v2 on v1

--- a/solution.py
+++ b/solution.py
@@ -50,31 +50,30 @@
     return jnp.stack([upper_half, lower_half]).astype(jnp.bfloat16)
 
 
-def toeplitz_kernel(taps_ref, forward_ref, adjoint_ref):
+def toeplitz_kernel(adjoint, taps_ref, out_ref):
     tap_count = taps_ref.shape[1]
     row_index = lax.broadcasted_iota(jnp.int32, (tap_count, tap_count), 0)
     col_index = lax.broadcasted_iota(jnp.int32, (tap_count, tap_count), 1)
+    taps = taps_ref[...].astype(jnp.float32)
     for index in range(taps_ref.shape[0]):
-        row = jnp.broadcast_to(taps_ref[index : index + 1, :], (tap_count, tap_count))
+        row = jnp.broadcast_to(taps[index : index + 1, :], (tap_count, tap_count))
         turned = pltpu.roll(row, 0, 1, stride=1, stride_axis=0)
         zeros = jnp.zeros_like(turned)
         near = jnp.where(col_index >= row_index, turned, zeros)
         far = jnp.where(col_index < row_index, turned, zeros)
-        forward_ref[index, :tap_count, :] = near.astype(jnp.bfloat16)
-        forward_ref[index, tap_count:, :] = far.astype(jnp.bfloat16)
-        adjoint_ref[index, :tap_count, :] = near.T.astype(jnp.bfloat16)
-        adjoint_ref[index, tap_count:, :] = far.T.astype(jnp.bfloat16)
-
-
-def toeplitz_tables(signatures):
+        near, far = (near.T, far.T) if adjoint else (near, far)
+        out_ref[index, :tap_count, :] = near.astype(jnp.bfloat16)
+        out_ref[index, tap_count:, :] = far.astype(jnp.bfloat16)
+
+
+def toeplitz_table(signatures, adjoint):
     count, tap_count = signatures.shape
-    shape = jax.ShapeDtypeStruct((count, 2 * tap_count, tap_count), jnp.bfloat16)
     return pl.pallas_call(
-        toeplitz_kernel,
-        out_shape=(shape, shape),
+        functools.partial(toeplitz_kernel, adjoint),
+        out_shape=jax.ShapeDtypeStruct((count, 2 * tap_count, tap_count), jnp.bfloat16),
         in_specs=[pl.BlockSpec(memory_space=pltpu.VMEM)],
-        out_specs=(pl.BlockSpec(memory_space=pltpu.VMEM),) * 2,
-    )(signatures.astype(jnp.float32))
+        out_specs=pl.BlockSpec(memory_space=pltpu.VMEM),
+    )(signatures)
 
 
 def apply_filter(traces, table, adjoint):
@@ -171,7 +170,8 @@
     trace_blocks = sample_count // tap_count
     capacity = max(2, 2 * shot_count // slab_count)
     slot_count = slab_count * rows_here * capacity
-    forward_tables, adjoint_tables = toeplitz_tables(signatures)
+    forward_tables = toeplitz_table(signatures, False)
+    adjoint_tables = toeplitz_table(signatures, True)
     flat_index = filter_index.reshape(-1)
     forward_table = forward_tables[flat_index]
     adjoint_table = adjoint_tables[flat_index]
@@ -546,11 +546,10 @@
     every_start = every_offset // tap_count % slab_blocks
     starts = jnp.sum(jnp.where(mine, every_start[:, None, :], 0), axis=2).reshape(-1)
     picks = jnp.sum(jnp.where(mine, every_pick[:, None, :], 0), axis=2).reshape(-1)
-    forward_tables, adjoint_tables = toeplitz_tables(signatures)
-
-    def correlate(blocks, model):
+    adjoint_tables = toeplitz_table(signatures, True)
+
+    def correlate(blocks, rim, model):
         low = blocks.astype(jnp.bfloat16)
-        rim = from_behind(low[: steps - 1], ("shot", "rep"), -1)
         extended = jnp.concatenate([low, rim, jnp.zeros_like(low[:1])], axis=0)
         return slots_to_spectra(
             starts, picks, extended, adjoint_tables, time_table_fixed, model, parts, slots
@@ -564,20 +563,24 @@
     def shrink_at(spectra, index, back, halves):
         level = lax.dynamic_slice_in_dim(thresholds[index], bin_start, bins)
         level = jnp.tile(level, local_rcv * rcv_count)[:, None]
-        return swap(
-            bins_stage(swap(spectra), slot_table, back, cosine, sine, level, place, halves)
-        )
+        return bins_stage(swap(spectra), slot_table, back, cosine, sine, level, place, halves)
 
     record_blocks = records.reshape(local_rcv, slab_blocks, tap_count).transpose(1, 0, 2)
-    spectra = shrink_at(correlate(record_blocks, None), 0, slot_table, 1)
+    rim = from_behind(record_blocks[: steps - 1].astype(jnp.bfloat16), ("shot", "rep"), -1)
+    spectra = shrink_at(correlate(record_blocks, rim, None), 0, slot_table, 1)
+    spectra, taps = lax.optimization_barrier((spectra, signatures))
+    forward_tables = toeplitz_table(taps, False)
     model, total = spectra_to_slab(
-        starts, picks, spectra, forward_tables, time_table_fixed, slab_blocks
-    )
-    carried = from_behind(total[slab_blocks : slab_blocks + steps - 1], ("shot", "rep"), 1)
-    blended = total[:slab_blocks].at[: steps - 1].add(carried)
-    left = record_blocks - blended
+        starts, picks, swap(spectra), forward_tables, time_table_fixed, slab_blocks
+    )
+    spill = total[slab_blocks : slab_blocks + steps - 1]
+    left = record_blocks - total[:slab_blocks]
+    carried = from_behind(spill, ("shot", "rep"), 1)
+    ahead = from_behind(left[: steps - 1], ("shot", "rep"), -1)
+    left = left.at[: steps - 1].add(-carried)
+    rim = (ahead - spill).astype(jnp.bfloat16)
     residual = left.transpose(1, 0, 2).reshape(local_rcv, slab_len)
-    spectra = shrink_at(correlate(left, model), 1, row_table, 2)
+    spectra = swap(shrink_at(correlate(left, rim, model), 1, row_table, 2))
     model = records_of(spectra, time_table_fixed, 2)
     return (model.reshape(rows_here, local_rcv, shot_count, NT), residual)
 

time: 176 us -> 176 us (level)
  blocking collectives: 31.6 us -> 0 us
  waiting for transfers between devices: 57.2 us -> 80.3 us
  starting transfers between devices: 30.9 us -> 39 us
    all_to_all x1 -> x0, blocking collectives: 31.6 us -> none  [swap(): return lax.all_to_all(value, everyone, 0, 0, tiled=True)]
    all_to_all x3 -> x4, waiting for transfers between devices: 53.8 us -> 75.1 us  [swap(): return lax.all_to_all(value, everyone, 0, 0, tiled=True)]
    all_to_all x3 -> x4, starting transfers between devices: 19.1 us -> 24.9 us  [swap(): return lax.all_to_all(value, everyone, 0, 0, tiled=True)]
    ppermute x3, starting transfers between devices: 5.44 us -> 7.78 us  [from_behind(): lax.ppermute(value, axis, [(source, source + steps) for source in range(f...]
    slice x4 -> x1, local copies, waits for them, and re-layouts: 2.04 us -> 0.01 us  [body_by_slots(): record_blocks[:steps - 1].astype(jnp.bfloat16)]
    unnamed x12 -> x14, local copies, waits for them, and re-layouts: 2.75 us -> 3.72 us
  transfers between devices with their start and end apart: 7 -> 8, of which waited for: 5 -> 7; matrix products, arithmetic and copies ran while one was open for 6% -> 5% of each run, Pallas kernels for 1% -> 2%
where the time goes in v2:
time: 176 us; the launch traced here: 175 us
  waiting for transfers between devices  80.3 us (46%)
  starting transfers between devices  39 us (22%)
  Pallas kernels  37.5 us (21%)
  local copies, waits for them, and re-layouts  8.85 us (5%)
  other arithmetic  6.91 us (4%)
    all_to_all x4, waiting for transfers between devices, swap(): return lax.all_to_all(value, everyone, 0, 0, tiled=True)  75.1 us
    all_to_all x4, starting transfers between devices, swap(): return lax.all_to_all(value, everyone, 0, 0, tiled=True)  24.9 us
    pallas_call x2, Pallas kernels, slots_to_spectra(): pl.pallas_call(functools.partial(analyse, model is not None), out_shape=j...  12.2 us
    pallas_call x2, Pallas kernels, bins_stage(): pl.pallas_call(functools.partial(bins_kernel, place, halves), out_shape=j...  12.1 us
    ppermute x3, starting transfers between devices, from_behind(): lax.ppermute(value, axis, [(source, source + steps) for source in range(f...  7.78 us
    pallas_call x1, Pallas kernels, spectra_to_slab(): pl.pallas_call(synthesise, out_shape=(jax.ShapeDtypeStruct((lanes // 2 *...  7.16 us
    all_to_all x1, starting transfers between devices, body_by_slots(): lax.all_to_all(jnp.broadcast_to(shots[None], (slab_count,) + shots.shape)...  6.35 us
    unnamed x14, local copies, waits for them, and re-layouts  3.72 us
  transfers between devices with their start and end apart: 8, of which 7 were waited for; matrix products, arithmetic and copies ran while one was open for 5% of the time, Pallas kernels for 2%

profile of v2, /device:TPU:0, one launch (start us, length us, event | category | flops | bytes accessed | tf_op | source)
XLA Modules:
  0.0 175.1 jit_solution(9196672602870873777)
XLA Ops:
  0.6 0.8 pad_add_fusion
  1.4 0.6 broadcast_in_dim.68
  2.0 6.4 %all-to-all-start = ((s32[8,2,1,32]{3,2,1,0:T(1,128)}), s32[8,2,1,32]{3,2,1,0:T(1,128)S(1)}, u32[]{:S(2)}, u32[]{:S(2)}) async-start(s32[8,2,1,32]{3,2,1,0:T(1,128)} %broadcast_in_dim.68), calls=%async_computation | async-start | bytes 16384 | tf_op jit(solution)/shard_map/all_to_all | solution.py:522
  8.5 1.3 collective-permute-start
  9.8 1.8 %shard_map.113.taps_ref = bf16[8,256,128]{2,1,0:T(8,128)(2,1)} custom-call(bf16[8,128]{1,0:T(8,128)(2,1)} %taps_ref.2), custom_call_target="tpu_custom_call" | custom-call | tf_op jit(solution)/shard_map/pallas_call | solution.py:71
  11.6 0.1 pad.7.clone
  11.6 2.3 %all-to-all-done = s32[8,2,1,32]{3,2,1,0:T(1,128)S(1)} async-done(((s32[8,2,1,32]{3,2,1,0:T(1,128)}), s32[8,2,1,32]{3,2,1,0:T(1,128)S(1)}, u32[]{:S(2)}, u32[]{:S(2)}) %all-to-all-start) | async-done | bytes 2080 | tf_op jit(solution)/shard_map/all_to_all | solution.py:522
  14.0 0.3 convert_reduce_fusion
  14.3 0.4 select_reduce_fusion.1
  14.7 0.6 reshape.273.starts_ref
  15.3 0.6 reshape.274.picks_ref
  15.9 1.0 maximum_maximum_fusion.blocks_ref
  16.9 5.7 %shard_map.114 = bf16[16,16,16,128]{3,2,1,0:T(8,128)(2,1)} custom-call(s32[64]{0:T(128)} %reshape.273.starts_ref, s32[64]{0:T(128)} %reshape.274.picks_ref, bf16[132,16,128]{2,1,0:T(8,128)(2,1)} %maximum_maximum_fusion.blocks_ref, bf16[8,256,128]{2,1,0:T(8,128)(2,1)} %shard_map.113.taps_ref, bf16[512,512]{1,0:T(8,128)(2,1)} %constant.109.clone.table_ref), custom_call_target="tpu_custom_call" | custom-call | tf_op jit(solution)/shard_map/pallas_call | solution.py:338
  22.7 4.7 %all-to-all-start.1 = ((bf16[16,16,16,128]{3,2,1,0:T(8,128)(2,1)}), bf16[16,16,16,128]{3,2,1,0:T(8,128)(2,1)S(1)}, u32[]{:S(2)}, u32[]{:S(2)}) async-start(bf16[16,16,16,128]{3,2,1,0:T(8,128)(2,1)} %shard_map.114), calls=%async_computation.1 | async-start | bytes 2097152 | tf_op jit(solution)/shard_map/all_to_all | solution.py:561
  27.4 0.1 fusion.10
  27.5 0.9 broadcast_in_dim_tile.8.level_ref
  28.4 1.2 select_reduce_fusion
  29.6 0.1 sub.25
  29.7 0.1 gt.16
  29.8 0.1 add_select_fusion
  29.9 0.1 select_n.71
  30.0 1.7 fusion.1.go_ref.back_ref
  31.7 18.6 %all-to-all-done.1.spectra_ref = bf16[16,16,16,128]{3,2,1,0:T(8,128)(2,1)S(1)} async-done(((bf16[16,16,16,128]{3,2,1,0:T(8,128)(2,1)}), bf16[16,16,16,128]{3,2,1,0:T(8,128)(2,1)S(1)}, u32[]{:S(2)}, u32[]{:S(2)}) %all-to-all-start.1) | async-done | bytes 1048608 | tf_op jit(solution)/shard_map/all_to_all | solution.py:561
  50.3 1.0 copy-done.3
  51.3 6.3 %shard_map.115 = bf16[16,16,16,128]{3,2,1,0:T(8,128)(2,1)} custom-call(bf16[16,16,16,128]{3,2,1,0:T(8,128)(2,1)} %copy-done.3, bf16[1024,512]{1,0:T(8,128)(2,1)} %fusion.1.go_ref.back_ref, bf16[1024,512]{1,0:T(8,128)(2,1)} %fusion.1.go_ref.back_ref, bf16[512,512]{1,0:T(8,128)(2,1)} %constant.112.clone.cosine_ref, bf16[512,512]{1,0:T(8,128)(2,1)} %constant.113.clone.sine_ref, ...), custom_call_target="tpu_custom_call" | custom-call | tf_op jit(solution)/shard_map/pallas_call | solution.py:478
  57.6 6.8 %all-to-all-start.2 = ((bf16[16,16,16,128]{3,2,1,0:T(8,128)(2,1)}), bf16[16,16,16,128]{3,2,1,0:T(8,128)(2,1)S(1)}, u32[]{:S(2)}, u32[]{:S(2)}) async-start(bf16[16,16,16,128]{3,2,1,0:T(8,128)(2,1)} %shard_map.115), calls=%async_computation.2 | async-start | bytes 2097152 | tf_op jit(solution)/shard_map/all_to_all | solution.py:561
  64.4 1.6 shard_map.116.taps_ref
  66.0 21.3 %all-to-all-done.2.spectra_ref = bf16[16,16,16,128]{3,2,1,0:T(8,128)(2,1)S(1)} async-done(((bf16[16,16,16,128]{3,2,1,0:T(8,128)(2,1)}), bf16[16,16,16,128]{3,2,1,0:T(8,128)(2,1)S(1)}, u32[]{:S(2)}, u32[]{:S(2)}) %all-to-all-start.2) | async-done | bytes 1048608 | tf_op jit(solution)/shard_map/all_to_all | solution.py:561
  87.2 1.0 copy-done.2
  88.2 7.2 %shard_map.117 = (f32[4096,128]{1,0:T(8,128)}, f32[132,16,128]{2,1,0:T(8,128)}) custom-call(s32[64]{0:T(128)} %reshape.273.starts_ref, s32[64]{0:T(128)} %reshape.274.picks_ref, bf16[16,16,16,128]{3,2,1,0:T(8,128)(2,1)} %copy-done.2, bf16[8,256,128]{2,1,0:T(8,128)(2,1)} %shard_map.116.taps_ref, bf16[512,512]{1,0:T(8,128)(2,1)} %constant.109.clone.table_ref), custom_call_target="tpu_custom_call" | custom-call | tf_op jit(solution)/shard_map/pallas_call | solution.py:399
  95.4 1.3 fusion.2
  96.7 1.3 collective-permute-start.2
  98.0 2.0 %collective-permute-done.2 = f32[3,16,128]{2,1,0:T(8,128)S(1)} collective-permute-done((f32[3,16,128]{2,1,0:T(8,128)S(1)}, f32[3,16,128]{2,1,0:T(8,128)S(1)}, u32[]{:S(2)}, u32[]{:S(2)}) %collective-permute-start.2) | collective-permute-done | bytes 24608 | tf_op jit(solution)/shard_map/ppermute | solution.py:18
  100.0 0.7 fusion.12
  100.7 5.2 %collective-permute-start.1 = (f32[3,16,128]{2,1,0:T(8,128)S(1)}, f32[3,16,128]{2,1,0:T(8,128)S(1)}, u32[]{:S(2)}, u32[]{:S(2)}) collective-permute-start(f32[3,16,128]{2,1,0:T(8,128)S(1)} %get-tuple-element.26), channel_id=1, source_target_pairs={{0,1},{1,4},{4,5},{5,8},{8,9},{9,12},{12,13},{2,3},{3,6},{6,7},{7,... | collective-permute-start | bytes 73736 | tf_op jit(solution)/shard_map/ppermute | solution.py:18
  106.0 0.8 collective-permute-done.1
  106.9 1.0 maximum_maximum_fusion.1.blocks_ref
  107.9 6.4 %shard_map.118 = bf16[16,16,16,128]{3,2,1,0:T(8,128)(2,1)} custom-call(s32[64]{0:T(128)} %reshape.273.starts_ref, s32[64]{0:T(128)} %reshape.274.picks_ref, bf16[132,16,128]{2,1,0:T(8,128)(2,1)} %maximum_maximum_fusion.1.blocks_ref, bf16[8,256,128]{2,1,0:T(8,128)(2,1)} %shard_map.113.taps_ref, bf16[512,512]{1,0:T(8,128)(2,1)} %constant.109.clone.table_ref, ...), custom_call_target="tpu_custom_call" | custom-call | tf_op jit(solution)/shard_map/pallas_call | solution.py:338
  114.3 6.6 %all-to-all-start.3 = ((bf16[16,16,16,128]{3,2,1,0:T(8,128)(2,1)}), bf16[16,16,16,128]{3,2,1,0:T(8,128)(2,1)S(1)}, u32[]{:S(2)}, u32[]{:S(2)}) async-start(bf16[16,16,16,128]{3,2,1,0:T(8,128)(2,1)} %shard_map.118), calls=%async_computation.3 | async-start | bytes 2097152 | tf_op jit(solution)/shard_map/all_to_all | solution.py:561
  120.9 0.9 broadcast_in_dim_tile.9.level_ref
  121.8 22.0 %all-to-all-done.3.spectra_ref = bf16[16,16,16,128]{3,2,1,0:T(8,128)(2,1)S(1)} async-done(((bf16[16,16,16,128]{3,2,1,0:T(8,128)(2,1)}), bf16[16,16,16,128]{3,2,1,0:T(8,128)(2,1)S(1)}, u32[]{:S(2)}, u32[]{:S(2)}) %all-to-all-start.3) | async-done | bytes 1048608 | tf_op jit(solution)/shard_map/all_to_all | solution.py:561
  143.8 1.0 copy-done.1
  144.8 5.8 %shard_map.119 = bf16[16,8,16,128]{3,2,1,0:T(8,128)(2,1)} custom-call(bf16[16,16,16,128]{3,2,1,0:T(8,128)(2,1)} %copy-done.1, bf16[1024,512]{1,0:T(8,128)(2,1)} %fusion.1.go_ref.back_ref, bf16[512,512]{1,0:T(8,128)(2,1)} %constant.111.clone.back_ref, bf16[512,512]{1,0:T(8,128)(2,1)} %constant.112.clone.cosine_ref, ...), custom_call_target="tpu_custom_call" | custom-call | tf_op jit(solution)/shard_map/pallas_call | solution.py:478
  150.5 6.8 %all-to-all-start.4 = ((bf16[16,8,16,128]{3,2,1,0:T(8,128)(2,1)}), bf16[16,8,16,128]{3,2,1,0:T(8,128)(2,1)S(1)}, u32[]{:S(2)}, u32[]{:S(2)}) async-start(bf16[16,8,16,128]{3,2,1,0:T(8,128)(2,1)} %shard_map.119), calls=%async_computation.4 | async-start | bytes 1048576 | tf_op jit(solution)/shard_map/all_to_all | solution.py:561
  157.3 1.0 copy_bitcast_fusion
  158.4 13.2 %all-to-all-done.4.spectra_ref = bf16[16,8,16,128]{3,2,1,0:T(8,128)(2,1)S(1)} async-done(((bf16[16,8,16,128]{3,2,1,0:T(8,128)(2,1)}), bf16[16,8,16,128]{3,2,1,0:T(8,128)(2,1)S(1)}, u32[]{:S(2)}, u32[]{:S(2)}) %all-to-all-start.4) | async-done | bytes 524320 | tf_op jit(solution)/shard_map/all_to_all | solution.py:561
  171.6 0.8 copy-done.4
  172.4 2.7 %shard_map.120 = f32[2,8,32,512]{3,2,1,0:T(8,128)} custom-call(bf16[16,8,16,128]{3,2,1,0:T(8,128)(2,1)} %copy-done.4, bf16[512,512]{1,0:T(8,128)(2,1)} %constant.109.clone.table_ref), custom_call_target="tpu_custom_call" | custom-call | tf_op jit(solution)/shard_map/pallas_call | solution.py:425
  (28 shorter events, 0.3 us)
Async XLA Ops:
  0.6 7.7 %copy-start = (f32[16,16384]{1,0:T(8,128)S(1)}, f32[16,16384]{1,0:T(8,128)}, u32[]{:S(2)}) copy-start(f32[16,16384]{1,0:T(8,128)} %param.12) | copy-start | bytes 3145732
  2.0 12.0 %all-to-all-start = ((s32[8,2,1,32]{3,2,1,0:T(1,128)}), s32[8,2,1,32]{3,2,1,0:T(1,128)S(1)}, u32[]{:S(2)}, u32[]{:S(2)}) async-start(s32[8,2,1,32]{3,2,1,0:T(1,128)} %broadcast_in_dim.68), calls=%async_computation | async-start | bytes 16384 | tf_op jit(solution)/shard_map/all_to_all | solution.py:522
  8.5 7.4 %collective-permute-start = (bf16[3,16,128]{2,1,0:T(8,128)(2,1)S(1)}, bf16[3,16,128]{2,1,0:T(8,128)(2,1)S(1)}, u32[]{:S(2)}, u32[]{:S(2)}) collective-permute-start(bf16[3,16,128]{2,1,0:T(8,128)(2,1)S(1)} %slice.57), channel_id=1, source_target_pairs={{1,0},{4,1},{5,4},{8,5},{9,8},{12,9},{13,12},{3,2},{6,3},{7,6},{10... | collective-permute-start | bytes 36872 | tf_op jit(solution)/shard_map/ppermute | solution.py:18
  16.9 10.5 %copy-start.5 = (f32[2,256]{1,0:T(2,128)S(1)}, f32[2,256]{1,0:T(2,128)}, u32[]{:S(2)}) copy-start(f32[2,256]{1,0:T(2,128)} %param.16) | copy-start | bytes 6148
  16.9 13.0 %copy-start.6 = (bf16[512,512]{1,0:T(8,128)(2,1)S(1)}, bf16[512,512]{1,0:T(8,128)(2,1)}, u32[]{:S(2)}) copy-start(bf16[512,512]{1,0:T(8,128)(2,1)} %constant.110.clone) | copy-start | bytes 1572868
  22.7 27.6 %all-to-all-start.1 = ((bf16[16,16,16,128]{3,2,1,0:T(8,128)(2,1)}), bf16[16,16,16,128]{3,2,1,0:T(8,128)(2,1)S(1)}, u32[]{:S(2)}, u32[]{:S(2)}) async-start(bf16[16,16,16,128]{3,2,1,0:T(8,128)(2,1)} %shard_map.114), calls=%async_computation.1 | async-start | bytes 2097152 | tf_op jit(solution)/shard_map/all_to_all | solution.py:561
  50.3 1.0 copy-start.3
  57.6 29.7 %all-to-all-start.2 = ((bf16[16,16,16,128]{3,2,1,0:T(8,128)(2,1)}), bf16[16,16,16,128]{3,2,1,0:T(8,128)(2,1)S(1)}, u32[]{:S(2)}, u32[]{:S(2)}) async-start(bf16[16,16,16,128]{3,2,1,0:T(8,128)(2,1)} %shard_map.115), calls=%async_computation.2 | async-start | bytes 2097152 | tf_op jit(solution)/shard_map/all_to_all | solution.py:561
  87.2 1.0 copy-start.2
  96.7 3.3 %collective-permute-start.2 = (f32[3,16,128]{2,1,0:T(8,128)S(1)}, f32[3,16,128]{2,1,0:T(8,128)S(1)}, u32[]{:S(2)}, u32[]{:S(2)}) collective-permute-start(f32[3,16,128]{2,1,0:T(8,128)S(1)} %slice.58), channel_id=1, source_target_pairs={{1,0},{4,1},{5,4},{8,5},{9,8},{12,9},{13,12},{3,2},{6,3},{7,6},{10... | collective-permute-start | bytes 73736 | tf_op jit(solution)/shard_map/ppermute | solution.py:18
  100.7 6.0 %collective-permute-start.1 = (f32[3,16,128]{2,1,0:T(8,128)S(1)}, f32[3,16,128]{2,1,0:T(8,128)S(1)}, u32[]{:S(2)}, u32[]{:S(2)}) collective-permute-start(f32[3,16,128]{2,1,0:T(8,128)S(1)} %get-tuple-element.26), channel_id=1, source_target_pairs={{0,1},{1,4},{4,5},{5,8},{8,9},{9,12},{12,13},{2,3},{3,6},{6,7},{7,... | collective-permute-start | bytes 73736 | tf_op jit(solution)/shard_map/ppermute | solution.py:18
  114.3 29.5 %all-to-all-start.3 = ((bf16[16,16,16,128]{3,2,1,0:T(8,128)(2,1)}), bf16[16,16,16,128]{3,2,1,0:T(8,128)(2,1)S(1)}, u32[]{:S(2)}, u32[]{:S(2)}) async-start(bf16[16,16,16,128]{3,2,1,0:T(8,128)(2,1)} %shard_map.118), calls=%async_computation.3 | async-start | bytes 2097152 | tf_op jit(solution)/shard_map/all_to_all | solution.py:561
  143.8 1.0 copy-start.1
  150.5 21.1 %all-to-all-start.4 = ((bf16[16,8,16,128]{3,2,1,0:T(8,128)(2,1)}), bf16[16,8,16,128]{3,2,1,0:T(8,128)(2,1)S(1)}, u32[]{:S(2)}, u32[]{:S(2)}) async-start(bf16[16,8,16,128]{3,2,1,0:T(8,128)(2,1)} %shard_map.119), calls=%async_computation.4 | async-start | bytes 1048576 | tf_op jit(solution)/shard_map/all_to_all | solution.py:561
  171.6 0.8 copy-start.4
